TPU v7x, 32 devices: a whole 2x2x4 slice. The times are simulated.
32 devices in a mesh: layer: 2 (over x), gx: 4 (over z), gy: 4 (over y, core).
Axes of the slice: x: 2, y: 2, z: 4, core: 2. Of those that a mesh axis runs over, the one named last changes fastest.
Arguments:
- pressure: float32 [16, 256, 1024], P('layer', 'gx', 'gy'), may hold values from -6 to 6
- source: float32 [16, 256, 1024], P('layer', 'gx', 'gy'), may hold values from -6 to 6
- perm_x: float32 [16, 256, 1024], P('layer', 'gx', 'gy'), may hold values from 0.05 to 0.5
- perm_y: float32 [16, 256, 1024], P('layer', 'gx', 'gy'), may hold values from 0.05 to 0.5
- line_inverse: float32 [2, 8, 8, 256, 1024], P('layer', None, None, 'gx', 'gy'), may hold values from -0.98 to 1.2
- robin_below: float32 [2, 256, 1024], P('layer', 'gx', 'gy'), may hold values from -6 to 6
- tile_count: int32 [2, 16], P('layer', ('gx', 'gy')), may hold values from 1 to 48, 256 in all within a row
- perf_owner: int32 [2, 768, 1], P('layer', ('gx', 'gy')), may hold values from 0 to 15; in each aligned block of 48 rows (0 to 47, 48 to 95, ..., all dimensions but the last counted through in order) at most 3 rows name the same one
- perf_well: int32 [2, 768], P('layer', ('gx', 'gy')), may hold values from 0 to 7
- perf_column: int32 [2, 768], P('layer', ('gx', 'gy')), may hold values from 0 to 16383
- perf_index: float32 [2, 768, 8], P('layer', ('gx', 'gy')), may hold values from 0.2 to 2
- well_rate: float32 [2, 128], P('layer', ('gx', 'gy')), may hold values from -8 to 8
Outputs:
- pressure_out: float32 [16, 256, 1024], P('layer', 'gx', 'gy')
- perf_flow: float32 [2, 768, 8], P('layer', ('gx', 'gy'))
Inputs may be any that keep to these rules, and one draw needn't show every extreme that they name: `tile_count`: live slots of a tile are its first ones; some tile of every group has all 48 live. `perf_owner`: among the 48 slots of one tile at most 3 name one owner.
All inputs are finite; a program needn't handle non-finite values.
Results may differ from a plain program's by a relative error of at most 0.00018.
Values sent between devices are 32-bit elements; how exact they have to be, the bound alone decides.
A program may use at most 64 MiB of HBM per device.

v0:
```python
import functools

import jax
import jax.numpy as jnp
from jax import lax
from jax.experimental import pallas as pl
from jax.experimental.pallas import tpu as pltpu
from jax.sharding import PartitionSpec as P

ITERS = 2
LIMIT = 24 << 20
MESH = pl.DeviceIdType.MESH
F32 = jnp.float32
BF16 = jnp.bfloat16
ROWS = 8
LANES = 128


def pieces(value):
    high = value.astype(BF16)
    rest = value - high.astype(F32)
    middle = rest.astype(BF16)
    low = (rest - middle.astype(F32)).astype(BF16)
    return jnp.concatenate([high, middle, low], axis=0)


def as_column(row):
    n = row.shape[1]
    eye = lax.broadcasted_iota(jnp.int32, (n, n), 0) == lax.broadcasted_iota(jnp.int32, (n, n), 1)
    return jnp.sum(jnp.where(eye, jnp.broadcast_to(row, (n, n)), 0.0), axis=1, keepdims=True)


def as_row(column):
    n = column.shape[0]
    eye = lax.broadcasted_iota(jnp.int32, (n, n), 0) == lax.broadcasted_iota(jnp.int32, (n, n), 1)
    return jnp.sum(jnp.where(eye, jnp.broadcast_to(column, (n, n)), 0.0), axis=0, keepdims=True)


def one_hots(column_row, width_x, width_y):
    slots = column_row.shape[1]
    column_col = as_column(column_row.astype(F32)).astype(jnp.int32)
    lane_x = lax.broadcasted_iota(jnp.int32, (slots, width_x), 1)
    in_x = (column_col >= lane_x * width_y) & (column_col < lane_x * width_y + width_y)
    x_of = jnp.sum(jnp.where(in_x, lane_x.astype(F32), 0.0), axis=1, keepdims=True).astype(jnp.int32)
    in_y = lax.broadcasted_iota(jnp.int32, (slots, width_y), 1) == column_col - x_of * width_y
    hot_x = jnp.where(in_x, 1.0, 0.0).astype(BF16)
    row_x = lax.broadcasted_iota(jnp.int32, (width_x, slots), 0)
    hot_xt = jnp.where(
        (column_row >= row_x * width_y) & (column_row < row_x * width_y + width_y), 1.0, 0.0
    ).astype(BF16)
    return in_y, jnp.concatenate([hot_x] * 3, axis=1), jnp.concatenate([hot_xt] * 3, axis=1)


def keep(field_in, flow_in, field_out, flow_out, sem):
    copies = [
        pltpu.make_async_copy(field_in, field_out, sem.at[0]),
        pltpu.make_async_copy(flow_in, flow_out, sem.at[1]),
    ]
    for copy in copies:
        copy.start()
    for copy in copies:
        copy.wait()


def kernel(
    dims,
    pressure,
    source,
    perm_x,
    perm_y,
    inverse,
    robin,
    count_in,
    owner_in,
    well_in,
    column_in,
    index_in,
    rate_in,
    field_out,
    flow_out,
    field,
    src,
    kx,
    ky,
    inv,
    lower,
    count_v,
    owner_v,
    well_v,
    column_v,
    index_v,
    rate_v,
    upper,
    rhs,
    solved,
    flow_v,
    halo_mult_x,
    halo_mult_y,
    well_send0,
    well_recv0,
    well_send1,
    well_recv1,
    row_send,
    row_recv,
    col_send,
    col_recv,
    coef_recv,
    down_send,
    down_recv,
    up_send,
    up_recv,
    own_down,
    spot_recv,
    delta_send,
    delta_recv,
    load_sem,
    store_sem,
    well_ssem,
    well_rsem,
    halo_ssem,
    halo_rsem,
    coef_ssem,
    coef_rsem,
    down_ssem,
    down_rsem,
    up_ssem,
    up_rsem,
    spot_ssem,
    spot_rsem,
    delta_ssem,
    delta_rsem,
):
    groups, n_gx, n_gy = dims
    tiles = n_gx * n_gy
    depth, width_x, width_y = field.shape
    slots = well_v.shape[1]
    own_wells = rate_v.shape[1]
    wells = tiles * own_wells
    me_l, me_x, me_y = lax.axis_index("layer"), lax.axis_index("gx"), lax.axis_index("gy")
    me = me_x * n_gy + me_y

    loads = [
        pltpu.make_async_copy(a, b, load_sem.at[i])
        for i, (a, b) in enumerate(
            [
                (pressure, field),
                (column_in, column_v),
                (well_in, well_v),
                (owner_in, owner_v),
                (index_in, index_v),
                (count_in, count_v),
                (rate_in, rate_v),
                (perm_x, kx),
                (perm_y, ky),
                (source, src),
                (robin, lower),
                (inverse, inv),
            ]
        )
    ]
    for load in loads:
        load.start()

    def peer(step):
        other = lax.rem(me + step, tiles)
        return {"gx": lax.div(other, n_gy), "gy": lax.rem(other, n_gy)}

    barrier = pltpu.get_barrier_semaphore()
    for step in range(1, tiles):
        pl.semaphore_signal(barrier, inc=1, device_id=peer(step), device_id_type=MESH)
    for step in range(1, groups):
        pl.semaphore_signal(
            barrier, inc=1, device_id={"layer": lax.rem(me_l + step, groups)}, device_id_type=MESH
        )

    for load in loads[1:7]:
        load.wait()
    live = lax.broadcasted_iota(jnp.int32, (slots, 1), 0) < count_v[...]
    in_y, hot_x3, hot_xt3 = one_hots(column_v[...], width_x, width_y)
    well_col = as_column(well_v[...].astype(F32)).astype(jnp.int32)
    owner_col = as_column(owner_v[...].astype(F32)).astype(jnp.int32)
    well_id = owner_col * own_wells + well_col
    member = jnp.where(
        (lax.broadcasted_iota(jnp.int32, (slots, wells), 1) == well_id) & live, 1.0, 0.0
    )
    layer_lane = lax.broadcasted_iota(jnp.int32, (slots, depth), 1)
    index = jnp.zeros((slots, depth), F32)
    for l in range(depth):
        index = jnp.where(layer_lane == l, as_column(index_v[l : l + 1, :]), index)
    rate_col = as_column(rate_v[...])
    rate_spot = (
        lax.broadcasted_iota(jnp.int32, (own_wells, wells), 1)
        == lax.broadcasted_iota(jnp.int32, (own_wells, wells), 0) + me * own_wells
    )
    rate_row = jnp.sum(jnp.where(rate_spot, rate_col, 0.0), axis=0, keepdims=True)

    def gathered(ref):
        at = jnp.zeros((slots, depth), F32)
        for l in range(depth):
            picked = jnp.dot(hot_x3, pieces(ref[l]), preferred_element_type=F32)
            one = jnp.sum(jnp.where(in_y, picked, 0.0), axis=1, keepdims=True)
            at = jnp.where(layer_lane == l, one, at)
        return at

    def well_row(at):
        share = jnp.sum(index * at, axis=1, keepdims=True)
        return jnp.sum(share * member, axis=0, keepdims=True) + rate_row

    def well_copy(it, step):
        send, recv = ((well_send0, well_recv0), (well_send1, well_recv1))[it]
        return pltpu.make_async_remote_copy(
            src_ref=send,
            dst_ref=recv.at[step],
            send_sem=well_ssem.at[it, step],
            recv_sem=well_rsem.at[it, step],
            device_id=peer(step),
            device_id_type=MESH,
        )

    sides = (
        ("gx", me_x, -1, me_x > 0),
        ("gx", me_x, 1, me_x < n_gx - 1),
        ("gy", me_y, -1, me_y > 0),
        ("gy", me_y, 1, me_y < n_gy - 1),
    )

    def halo_copy(it, side):
        axis, mine, way, _ = sides[side]
        send, recv = (row_send, row_recv) if side < 2 else (col_send, col_recv)
        width = slice(0, 2 if it == 0 else 1)
        if side < 2:
            source_ref = send.at[it, side, width]
            target_ref = recv.at[it, 1 - side, width]
        else:
            source_ref = send.at[it, side - 2]
            target_ref = recv.at[it, 3 - side]
        return pltpu.make_async_remote_copy(
            src_ref=source_ref,
            dst_ref=target_ref,
            send_sem=halo_ssem.at[it, side],
            recv_sem=halo_rsem.at[it, side ^ 1],
            device_id={axis: mine + way},
            device_id_type=MESH,
        )

    def halo_landing(it, side):
        axis, mine, way, _ = sides[side]
        if side < 2:
            width = slice(0, 2 if it == 0 else 1)
            ref, other = row_recv.at[it, side, width], row_send.at[it, 1 - side, width]
        else:
            ref, other = col_recv.at[it, side - 2], col_send.at[it, 3 - side]
        return pltpu.make_async_remote_copy(
            src_ref=other,
            dst_ref=ref,
            send_sem=halo_ssem.at[it, side],
            recv_sem=halo_rsem.at[it, side],
            device_id={axis: mine + way},
            device_id_type=MESH,
        )

    lane128 = lax.broadcasted_iota(jnp.int32, (width_x, 128), 1)

    def packed_columns(arrays, lane):
        out = jnp.zeros((width_x, 128), F32)
        at = 0
        for ref in arrays:
            for l in range(depth):
                out = jnp.where(lane128 == at, ref[l, :, lane : lane + 1], out)
                at += 1
        return out

    def stage_halos(it):
        for l in range(depth):
            row_send[it, 0, 0, l : l + 1, :] = field[l, 0:1, :]
            row_send[it, 1, 0, l : l + 1, :] = field[l, width_x - 1 : width_x, :]
            if it == 0:
                row_send[it, 0, 1, l : l + 1, :] = kx[l, 0:1, :]
                row_send[it, 1, 1, l : l + 1, :] = kx[l, width_x - 1 : width_x, :]
        arrays = (field, ky) if it == 0 else (field,)
        col_send[it, 0] = packed_columns(arrays, 0)
        col_send[it, 1] = packed_columns(arrays, width_y - 1)
        for side in range(4):

            @pl.when(jnp.logical_not(sides[side][3]))
            def _():
                if side < 2:
                    row_recv[it, side] = jnp.zeros(row_recv.shape[2:], F32)
                else:
                    col_recv[it, side - 2] = jnp.zeros(col_recv.shape[2:], F32)

    def start_halos(it):
        for side in range(4):
            @pl.when(sides[side][3])
            def _():
                halo_copy(it, side).start()

    def wait_halos(it):
        for side in range(4):
            @pl.when(sides[side][3])
            def _():
                halo_landing(it, side).wait_recv()

    last_x = lax.broadcasted_iota(jnp.int32, (width_x, width_y), 0) == width_x - 1
    first_x = lax.broadcasted_iota(jnp.int32, (width_x, width_y), 0) == 0
    last_y = lax.broadcasted_iota(jnp.int32, (width_x, width_y), 1) == width_y - 1
    first_y = lax.broadcasted_iota(jnp.int32, (width_x, width_y), 1) == 0

    def face_coefficients():
        for l in range(depth):
            mult = kx[l]
            kx[l] = 0.5 * (mult + pltpu.roll(mult, width_x - 1, 0))
            mult = ky[l]
            ky[l] = 0.5 * (mult + pltpu.roll(mult, width_y - 1, 1))

    def edge_coefficients():
        for l in range(depth):
            one = slice(l, l + 1)
            halo_mult_x[one, :] = 0.5 * (row_send[0, 0, 1, one, :] + row_recv[0, 0, 1, one, :])
            kx[l, width_x - 1 : width_x, :] = 0.5 * (
                row_send[0, 1, 1, one, :] + row_recv[0, 1, 1, one, :]
            )
            lane = slice(depth + l, depth + l + 1)
            ky[l, :, width_y - 1 : width_y] = 0.5 * (
                col_send[0, 1, :, lane] + col_recv[0, 1, :, lane]
            )
        halo_mult_y[...] = 0.5 * (col_send[0, 0] + col_recv[0, 0])

    def lateral_sum():
        for l in range(depth):
            now = field[l]
            face_x, face_y = kx[l], ky[l]
            east = jnp.where(last_x, 0.0, face_x * pltpu.roll(now, width_x - 1, 0))
            west = jnp.where(first_x, 0.0, pltpu.roll(face_x * now, 1, 0))
            north = jnp.where(last_y, 0.0, face_y * pltpu.roll(now, width_y - 1, 1))
            south = jnp.where(first_y, 0.0, pltpu.roll(face_y * now, 1, 1))
            rhs[l] = src[l] + ((east + west) + (north + south))

    def lateral_edges(it):
        end_x, end_y = slice(width_x - 1, width_x), slice(width_y - 1, width_y)
        for l in range(depth):
            one = slice(l, l + 1)
            lane = slice(depth + l, depth + l + 1)
            rhs[l, 0:1, :] += halo_mult_x[one, :] * row_recv[it, 0, 0, one, :]
            rhs[l, end_x, :] += kx[l, end_x, :] * row_recv[it, 1, 0, one, :]
            rhs[l, :, 0:1] += halo_mult_y[:, lane] * col_recv[it, 0, :, one]
            rhs[l, :, end_y] += ky[l, :, end_y] * col_recv[it, 1, :, one]

    def layer_copy(ref, target, ssem, rsem, other):
        return pltpu.make_async_remote_copy(
            src_ref=ref,
            dst_ref=target,
            send_sem=ssem,
            recv_sem=rsem,
            device_id={"layer": other},
            device_id_type=MESH,
        )

    last = depth - 1
    coef_at = ((0, 0), (0, last), (last, 0))[: 1 if groups == 2 else 3]

    def coef_copy(which, sender, other):
        i, j = coef_at[which]
        return layer_copy(
            inv.at[i, j],
            coef_recv.at[sender, which],
            coef_ssem.at[other, which],
            coef_rsem.at[sender, which],
            other,
        )

    def coef_sent(which, sender, other):
        if which == 0:
            return other < sender
        if which == 1:
            return other < sender < groups - 1
        return 0 < sender < groups - 1

    def spot_copy(step):
        return layer_copy(
            column_v, spot_recv.at[step], spot_ssem.at[step], spot_rsem.at[step],
            lax.rem(me_l + step, groups),
        )

    def delta_copy(it, step):
        return layer_copy(
            delta_send.at[it], delta_recv.at[it, step], delta_ssem.at[it, step],
            delta_rsem.at[it, step], lax.rem(me_l + step, groups),
        )

    def down_copy(it, sender, other):
        return layer_copy(
            down_send.at[it], down_recv.at[it, sender], down_ssem.at[it, other],
            down_rsem.at[it, sender], other,
        )

    def up_copy(it, sender, other):
        return layer_copy(
            up_send.at[it], up_recv.at[it, sender], up_ssem.at[it, other],
            up_rsem.at[it, sender], other,
        )

    def layer_sends(act, which):
        for g in range(groups):

            @pl.when(me_l == g)
            def _():
                for other in range(groups):
                    if other == g:
                        continue
                    if which == "coef":
                        for c in range(len(coef_at)):
                            if coef_sent(c, g, other):
                                getattr(coef_copy(c, g, other), act)()
                    else:
                        it = which
                        if g < groups - 1:
                            getattr(down_copy(it, g, other), act)()
                        if other < g:
                            getattr(up_copy(it, g, other), act)()

    def chunk_loop(body):
        def step(c, carry):
            body(pl.ds(pl.multiple_of(c * ROWS, ROWS), ROWS))
            return carry

        lax.fori_loop(0, width_x // ROWS, step, 0)

    def dot_layer(i, rows, terms):
        total = inv[i, 0, rows, :] * terms[0]
        for j in range(1, depth):
            total = total + inv[i, j, rows, :] * terms[j]
        return total

    def solve_faces(it):
        def body(rows):
            terms = [rhs[j, rows, :] for j in range(depth)]
            bottom = dot_layer(last, rows, terms)
            top = dot_layer(0, rows, terms)
            below = lower[rows, :]
            nothing = jnp.zeros_like(below)
            down_send[it, rows, :] = inv[last, 0, rows, :] * nothing + (
                (bottom + inv[last, last, rows, :] * below) - below
            )
            up_send[it, rows, :] = inv[0, last, rows, :] * nothing + top

        chunk_loop(body)

    def solve_all():
        def body(rows):
            terms = [rhs[j, rows, :] for j in range(depth)]
            for i in range(depth):
                value = dot_layer(i, rows, terms)
                solved[i, rows, :] = value
                if i == last:
                    below = lower[rows, :]
                    own_down[rows, :] = inv[last, 0, rows, :] * jnp.zeros_like(below) + (
                        (value + inv[last, last, rows, :] * below) - below
                    )

        chunk_loop(body)

    def sweeps(it):
        for g in range(groups):

            @pl.when(me_l == g)
            def _():
                for k in range(groups):
                    if k == g:
                        continue
                    if k < groups - 1:
                        down_copy(it, k, k).wait_recv()
                    if k > g:
                        up_copy(it, k, k).wait_recv()
                    if it == 0:
                        for c in range(len(coef_at)):
                            if coef_sent(c, k, g):
                                coef_copy(c, k, k).wait_recv()
                    step = (g - k) % groups
                    delta_copy(it, step).wait_recv()
                    other_y, _, other_xt3 = spots[step]
                    for row, wanted, ref in ((0, k < groups - 1, down_recv), (1, k > g, up_recv)):
                        if wanted:
                            spread = as_column(delta_recv[it, step, row : row + 1, :])
                            spread = pieces(jnp.where(other_y, spread, 0.0))
                            ref[it, k] = ref[it, k] + jnp.dot(
                                other_xt3, spread, preferred_element_type=F32
                            )

                def body(rows):
                    def coef(which, k):
                        i, j = coef_at[which]
                        return inv[i, j, rows, :] if k == g else coef_recv[k, which, rows, :]

                    above = [jnp.zeros((ROWS, width_y), F32)]
                    for k in range(groups - 1):
                        value = own_down[rows, :] if k == g else down_recv[it, k, rows, :]
                        if k > 0:
                            value = coef(2, k) * above[k] + value
                        above.append(value)
                    below = jnp.zeros((ROWS, width_y), F32)
                    for k in range(groups - 1, g, -1):
                        value = (up_recv[it, k, rows, :] + coef(0, k) * above[k]) - above[k]
                        if k < groups - 1:
                            value = coef(1, k) * below + value
                        below = value
                    upper[rows, :] = above[g]
                    lower[rows, :] = below

                chunk_loop(body)

    def update():
        def body(rows):
            above, below = upper[rows, :], lower[rows, :]
            for i in range(depth):
                field[i, rows, :] = (
                    solved[i, rows, :]
                    + inv[i, 0, rows, :] * above
                    + inv[i, last, rows, :] * below
                )

        chunk_loop(body)

    index_total = None
    spots = [None] * groups
    for it in range(ITERS):
        if it == 0:
            loads[0].wait()
        at = gathered(field)
        if it == 0:
            index_row = jnp.sum(
                jnp.sum(index, axis=1, keepdims=True) * member, axis=0, keepdims=True
            )
            well_send0[...] = jnp.concatenate([well_row(at), index_row], axis=1)
            loads[7].wait()
            loads[8].wait()
            stage_halos(it)
            pl.semaphore_wait(barrier, tiles - 1 + groups - 1)
        else:
            well_send1[...] = well_row(at)
        for step in range(1, tiles):
            well_copy(it, step).start()
        if it > 0:
            stage_halos(it)
        start_halos(it)
        if it == 0:
            for step in range(1, groups):
                spot_copy(step).start()
            for load in loads[9:]:
                load.wait()
            layer_sends("start", "coef")
        if it == 0:
            face_coefficients()
        lateral_sum()
        wait_halos(it)
        if it == 0:
            edge_coefficients()
        lateral_edges(it)
        solve_faces(it)
        layer_sends("start", it)
        if it == 0:
            for step in range(1, groups):
                spot_copy(step).wait_recv()
                spots[step] = one_hots(spot_recv[step], width_x, width_y)
            face_last, face_first = gathered(inv.at[last]), gathered(inv.at[0])
        total = (well_send0, well_send1)[it][...]
        for step in range(1, tiles):
            well_copy(it, step).wait_recv()
        for step in range(1, tiles):
            total = total + (well_recv0, well_recv1)[it][step]
        if it == 0:
            index_total = total[:, wells:] + 1.0
            total = total[:, :wells]
        bottom_hole = total / index_total
        hole = jnp.sum(member * bottom_hole, axis=1, keepdims=True)
        flow = jnp.where(live, index * (hole - at), 0.0)
        for row, face in enumerate((face_last, face_first)):
            delta_send[it, row : row + 1, :] = as_row(
                jnp.sum(face * flow, axis=1, keepdims=True)
            )
        for step in range(1, groups):
            delta_copy(it, step).start()
        if it == ITERS - 1:
            for l in range(depth):
                flow_v[l : l + 1, :] = as_row(flow[:, l : l + 1])
            flow_store = pltpu.make_async_copy(flow_v, flow_out, store_sem.at[0])
            flow_store.start()
        for l in range(depth):
            spread = jnp.where(in_y, flow[:, l : l + 1], 0.0)
            rhs[l] = rhs[l] + jnp.dot(hot_xt3, pieces(spread), preferred_element_type=F32)
        solve_all()
        sweeps(it)
        update()
    field_store = pltpu.make_async_copy(field, field_out, store_sem.at[1])
    field_store.start()
    for it in range(ITERS):
        for step in range(1, tiles):
            well_copy(it, step).wait_send()
        for side in range(4):

            @pl.when(sides[side][3])
            def _():
                halo_copy(it, side).wait_send()

        layer_sends("wait_send", it)
        for step in range(1, groups):
            delta_copy(it, step).wait_send()
    for step in range(1, groups):
        spot_copy(step).wait_send()
    layer_sends("wait_send", "coef")
    flow_store.wait()
    field_store.wait()


def split(value, count):
    out = []
    for _ in range(count - 1):
        part = value.astype(BF16).astype(F32)
        out.append(part)
        value = value - part
    out.append(value)
    return out


def fused(
    dims,
    pressure,
    source,
    perm_x,
    perm_y,
    inverse,
    robin,
    count_in,
    owner_in,
    well_in,
    column_in,
    index_in,
    rate_in,
    field,
    flow_out,
    src,
    kx,
    ky,
    inv,
    lower,
    column_s,
    count_v,
    owner_v,
    well_v,
    column_v,
    index_v,
    rate_v,
    slabs,
    lower_at,
    rhs,
    solved,
    spread,
    left,
    own,
    par,
    lines,
    at_send,
    at_recv,
    coef_x,
    coef_y,
    well_send0,
    well_recv0,
    well_send1,
    well_recv1,
    row_send,
    row_recv,
    col_send,
    col_recv,
    gain_x,
    gain_y,
    gain_xr,
    gain_yr,
    edge_send,
    edge_recv,
    x_send,
    x_recv,
    kappa,
    smem_sem,
    slab_sem,
    load_sem,
    rest_sem,
    well_ssem,
    well_rsem,
    halo_ssem,
    halo_rsem,
    gain_ssem,
    gain_rsem,
    edge_ssem,
    edge_rsem,
    x_ssem,
    x_rsem,
    misc_ssem,
    misc_rsem,
):
    groups, n_gx, n_gy, depth = dims
    tiles = n_gx * n_gy
    width_x, width_y = lower.shape
    slots = well_v.shape[1]
    own_wells = rate_v.shape[1]
    wells = tiles * own_wells
    me_l, me_x, me_y = lax.axis_index("layer"), lax.axis_index("gx"), lax.axis_index("gy")
    me = me_x * n_gy + me_y
    upper_group = me_l == 0
    phi = (1 - me_l) * (depth - 1)
    halves = width_y // LANES

    def sheet(i):
        return slice(i * width_x, (i + 1) * width_x)

    def dyn_sheet(i):
        return pl.ds(pl.multiple_of(i * width_x, width_x), width_x)

    def peer(dl, step):
        return {"layer": me_l ^ dl, "gx": me_x ^ (step // n_gy), "gy": me_y ^ (step % n_gy)}

    peers = [
        (dl, step)
        for step in reversed(range(tiles))
        for dl in reversed(range(groups))
        if (dl, step) != (0, 0)
    ]
    partner = {"layer": 1 - me_l}

    block = depth * width_x
    to_smem = pltpu.make_async_copy(column_in, column_s, smem_sem)
    to_smem.start()
    loads = [
        pltpu.make_async_copy(a, b, load_sem.at[i])
        for i, (a, b) in enumerate(
            [
                (column_in, column_v),
                (well_in, well_v),
                (owner_in, owner_v),
                (index_in, index_v),
                (count_in, count_v),
                (rate_in, rate_v),
                (pressure, field),
                (perm_x, kx),
                (perm_y, ky),
                (source, src),
                (robin, lower),
            ]
        )
    ]
    tiled = [
        pltpu.make_async_copy(pressure.at[:, n * LANES : (n + 1) * LANES], slabs.at[n], slab_sem)
        for n in range(halves)
    ]
    barrier = pltpu.get_barrier_semaphore()
    for load in loads[:6] + tiled:
        load.start()
    for dl, step in peers:
        pl.semaphore_signal(barrier, inc=1, device_id=peer(dl, step), device_id_type=MESH)
    face_block = pl.ds(pl.multiple_of(phi * block, block), block)
    other_blocks = pl.ds(pl.multiple_of(me_l * block, block), (depth - 1) * block)

    def line_loads(rows, sem):
        return [
            pltpu.make_async_copy(
                inverse.at[rows, n * LANES : (n + 1) * LANES], inv.at[n, rows, :], sem
            )
            for n in range(halves)
        ]

    def lines_loaded(rows, sem):
        return pltpu.make_async_copy(inv.at[:, rows, :], inv.at[:, rows, :], sem)

    for load in loads[6:] + line_loads(face_block, rest_sem.at[0]):
        load.start()

    lane = lax.broadcasted_iota(jnp.int32, (8, LANES), 1)
    sub = lax.broadcasted_iota(jnp.int32, (8, LANES), 0)

    own[...] = jnp.zeros(own.shape, F32)
    for load in loads[:6]:
        load.wait()
    live = lax.broadcasted_iota(jnp.int32, (depth, slots), 1) < count_v[...]
    own[0:depth, 0:slots] = jnp.where(live, index_v[...], 0.0)
    own[2 * depth : 2 * depth + 1, 0:slots] = column_v[...].astype(F32)
    own[2 * depth + 1 : 2 * depth + 2, 0:slots] = (owner_v[...] * own_wells + well_v[...]).astype(F32)
    index = own[0:depth, :]
    well_id = own[2 * depth + 1 : 2 * depth + 2, :]
    member = jnp.where(
        lax.broadcasted_iota(jnp.int32, (LANES, wells), 1).astype(F32) == as_column(well_id), 1.0, 0.0
    ).astype(BF16)
    rate_col = as_column(rate_v[...])
    rate_spot = (
        lax.broadcasted_iota(jnp.int32, (own_wells, wells), 1)
        == lax.broadcasted_iota(jnp.int32, (own_wells, wells), 0) + me * own_wells
    )
    rate_row = jnp.sum(jnp.where(rate_spot, rate_col, 0.0), axis=0, keepdims=True)

    def gather(jobs, span):
        shift = width_y.bit_length() - 1

        def step(c, accs):
            for k in range(span):
                s = c * span + k
                column = column_s[0, s]
                if width_y == 1 << shift:
                    x, y = lax.shift_right_logical(column, shift), column & (width_y - 1)
                else:
                    x, y = lax.div(column, width_y), lax.rem(column, width_y)
                tile = lax.shift_right_logical(y, LANES.bit_length() - 1)
                turn = (s + LANES - (y & (LANES - 1))) & (LANES - 1)
                found = []
                for ref, first, stride, count in jobs:
                    if count == 1:
                        value = ref[tile, pl.ds(first + x, 1), :]
                    else:
                        value = ref[tile, pl.ds(first + x, count, stride=stride), :]
                    found.append(pltpu.roll(value, turn, 1))
                accs = tuple(
                    jnp.where(lane[: value.shape[0]] == s, value, acc) for acc, value in zip(accs, found)
                )
            return accs

        accs = tuple(jnp.zeros((count, LANES), F32) for _, _, _, count in jobs)
        if span == slots:
            return step(0, accs)
        return lax.fori_loop(0, slots // span, step, accs)

    wide = lax.broadcasted_iota(jnp.int32, (16, LANES), 0)

    def binned(rows):
        at, out = 0, jnp.zeros((16, LANES), F32)
        for row in rows:
            for part in split(row, 3):
                out = jnp.where(wide == at, part, out)
                at += 1
        total = jnp.dot(out.astype(BF16), member, preferred_element_type=F32)
        return [jnp.sum(total[3 * k : 3 * k + 3, :], axis=0, keepdims=True) for k in range(len(rows))]

    def remote(a, b, ssem, rsem, device):
        return pltpu.make_async_remote_copy(
            src_ref=a, dst_ref=b, send_sem=ssem, recv_sem=rsem, device_id=device, device_id_type=MESH
        )

    def well_copy(it, dl, step):
        send, recv = ((well_send0, well_recv0), (well_send1, well_recv1))[it]
        return remote(
            send, recv.at[dl * tiles + step - 1], well_ssem.at[it], well_rsem.at[it], peer(dl, step)
        )

    def all_wells(it):
        recv = (well_recv0, well_recv1)[it]
        return remote(recv, recv, well_ssem.at[it], well_rsem.at[it], partner)

    sides = (
        ("gx", me_x, -1, me_x > 0),
        ("gx", me_x, 1, me_x < n_gx - 1),
        ("gy", me_y, -1, me_y > 0),
        ("gy", me_y, 1, me_y < n_gy - 1),
    )

    def across(side, flip=False):
        axis, mine, way, _ = sides[side]
        out = {axis: mine + way}
        if flip:
            out["layer"] = 1 - me_l
        return out

    def halo_copy(it, side, landing=False):
        other = side ^ 1
        at, to = (other, side) if landing else (side, other)
        width = slice(0, 2 if it == 0 else 1)
        if side < 2:
            a, b = row_send.at[it, at, width], row_recv.at[it, to, width]
        else:
            a, b = col_send.at[it, at - 2], col_recv.at[it, to - 2]
        return remote(a, b, halo_ssem.at[it, at], halo_rsem.at[it, to], across(side))

    def gain_copy(side, landing=False):
        other = side ^ 1
        at, to = (other, side) if landing else (side, other)
        if side < 2:
            a, b = gain_x.at[at], gain_xr.at[to]
        else:
            a, b = gain_y.at[at - 2], gain_yr.at[to - 2]
        return remote(a, b, gain_ssem.at[at], gain_rsem.at[to], across(side))

    def edge_copy(side, landing=False):
        other = side ^ 1
        at, to = (other, side) if landing else (side, other)
        return remote(
            edge_send.at[1, at], edge_recv.at[1, to], edge_ssem.at[at], edge_rsem.at[to],
            across(side, True),
        )

    def edge_pack():
        return remote(edge_send.at[0], edge_recv.at[0], edge_ssem.at[4], edge_rsem.at[4], partner)

    def x_copy(it):
        return remote(x_send.at[it], x_recv.at[it], x_ssem.at[it], x_rsem.at[it], partner)

    slot_copy = remote(own, par, misc_ssem.at[0], misc_rsem.at[0], partner)
    at_copy = remote(at_send, at_recv, misc_ssem.at[1], misc_rsem.at[1], partner)
    kappa_copy = remote(inv.at[:, 0:width_x, :], kappa, misc_ssem.at[2], misc_rsem.at[2], partner)

    lane_x = lax.broadcasted_iota(jnp.int32, (width_x, LANES), 1)

    def packed_columns(blocks, y):
        out = jnp.zeros((width_x, LANES), F32)
        for at, (ref, rows) in enumerate(blocks):
            tile = y - y % LANES
            value = ref[rows, tile : tile + LANES]
            out = jnp.where(lane_x == at, pltpu.roll(value, (at - y) % LANES, 1), out)
        return out

    def each(ref):
        return [(ref, sheet(l)) for l in range(depth)]

    ends_x, ends_y = (0, width_x - 1), (0, width_y - 1)

    def stage_halos(it):
        for side, x in enumerate(ends_x):
            for l in range(depth):
                row = l * width_x + x
                row_send[it, side, 0, l : l + 1, :] = field[row : row + 1, :]
                if it == 0:
                    row_send[it, side, 1, l : l + 1, :] = kx[row : row + 1, :]
        blocks = each(field) + (each(ky) if it == 0 else [])
        for side, y in enumerate(ends_y):
            col_send[it, side] = packed_columns(blocks, y)

    def clear_halos(it):
        for side in range(4):

            @pl.when(jnp.logical_not(sides[side][3]))
            def _():
                if side < 2:
                    row_recv[it, side] = jnp.zeros(row_recv.shape[2:], F32)
                else:
                    col_recv[it, side - 2] = jnp.zeros(col_recv.shape[2:], F32)
                if it == 1:
                    edge_recv[it, side] = jnp.zeros(edge_recv.shape[2:], F32)

    def on_sides(body):
        for side in range(4):
            pl.when(sides[side][3])(functools.partial(body, side))

    first_x = lax.broadcasted_iota(jnp.int32, (width_x, width_y), 0) == width_x - 1
    first_y = lax.broadcasted_iota(jnp.int32, (width_x, width_y), 1) == width_y - 1

    def face_coefficients():
        for l in range(depth):
            mult = kx[sheet(l), :]
            kx[sheet(l), :] = jnp.where(first_x, 0.0, 0.5 * (mult + pltpu.roll(mult, width_x - 1, 0)))
            mult = ky[sheet(l), :]
            ky[sheet(l), :] = jnp.where(first_y, 0.0, 0.5 * (mult + pltpu.roll(mult, width_y - 1, 1)))

    def lateral_sum():
        for l in range(depth):
            now = field[sheet(l), :]
            face_x, face_y = kx[sheet(l), :], ky[sheet(l), :]
            east = face_x * pltpu.roll(now, width_x - 1, 0)
            west = pltpu.roll(face_x * now, 1, 0)
            north = face_y * pltpu.roll(now, width_y - 1, 1)
            south = pltpu.roll(face_y * now, 1, 1)
            rhs[sheet(l), :] = src[sheet(l), :] + ((east + west) + (north + south))

    def lateral_edges(it):
        for l in range(depth):
            one = slice(l, l + 1)
            for side, x in enumerate(ends_x):
                row = slice(l * width_x + x, l * width_x + x + 1)
                rhs[row, :] += coef_x[side, one, :] * row_recv[it, side, 0, one, :]
        for side, y in enumerate(ends_y):
            tile = y - y % LANES
            terms = coef_y[side] * col_recv[it, side]
            for l in range(depth):
                term = pltpu.roll(terms, (y - l) % LANES, 1)
                rhs[sheet(l), tile : tile + LANES] += jnp.where(lane_x == y - tile, term, 0.0)

    def edge_coefficients():
        for side in range(2):
            coef_x[side] = 0.5 * (row_send[0, side, 1] + row_recv[0, side, 1])
            coef_y[side] = pltpu.roll(
                0.5 * (col_send[0, side] + col_recv[0, side]), LANES - depth, 1
            )

    def chunk_loop(body):
        def step(c, carry):
            body(pl.multiple_of(c * ROWS, ROWS))
            return carry

        lax.fori_loop(0, width_x // ROWS, step, 0)

    def whole(ref, rows):
        return jnp.concatenate([ref[n, rows, :] for n in range(halves)], axis=1)

    def rows_of(i, at):
        return pl.ds(pl.multiple_of(i * width_x + at, ROWS), ROWS)

    def own_face(at):
        below = lower[pl.ds(at, ROWS), :]
        corner = whole(inv, rows_of(phi * depth + phi, at))
        return jnp.where(upper_group, corner * below - below, 0.0)

    def interior_face(it):
        def body(at):
            total = own_face(at)
            for j in range(depth):
                total = total + whole(inv, rows_of(phi * depth + j, at)) * rhs[rows_of(j, at), :]
            x_send[it, pl.ds(at, ROWS), :] = total

        chunk_loop(body)

    def solve_all():
        def body(at):
            terms = [rhs[rows_of(j, at), :] for j in range(depth)]
            for i in range(depth):
                total = whole(inv, rows_of(i * depth, at)) * terms[0]
                for j in range(1, depth):
                    total = total + whole(inv, rows_of(i * depth + j, at)) * terms[j]
                for n in range(halves):
                    solved[n, rows_of(i, at), :] = total[:, n * LANES : (n + 1) * LANES]

        chunk_loop(body)

    def robin_data(it):
        for side, x in enumerate(ends_x):
            x_recv[it, x : x + 1, :] += edge_recv[it, side]
        for side, y in enumerate(ends_y):
            x_recv[it, :, y : y + 1] += as_column(edge_recv[it, 2 + side, :, 0:width_x])

        def body(at):
            rows = pl.ds(at, ROWS)
            mine = whole(solved, rows_of(phi, at)) + own_face(at)
            data = x_recv[it, rows, :] + jnp.where(upper_group, whole(kappa, rows) * mine - mine, 0.0)
            lower[rows, :] = data
            for n in range(halves):
                lower_at[n, rows, :] = data[:, n * LANES : (n + 1) * LANES]

        chunk_loop(body)

    def update():
        def body(at):
            rows = pl.ds(at, ROWS)
            data = lower[rows, :] + spread[rows_of(depth, at), :]
            lower[rows, :] = data
            for i in range(depth):
                field[rows_of(i, at), :] = (
                    whole(solved, rows_of(i, at))
                    + spread[rows_of(i, at), :]
                    + whole(inv, rows_of(i * depth + phi, at)) * data
                )

        chunk_loop(body)

    def start(copy):
        copy.start()

    to_smem.wait()
    pltpu.make_async_copy(slabs, slabs, slab_sem).wait()
    for load in line_loads(other_blocks, rest_sem.at[1]):
        load.start()
    at_own = gather([(slabs, 0, width_x, depth)], slots)[0]
    own[depth : 2 * depth, :] = at_own
    share, sums = binned(
        [jnp.sum(index * at_own, axis=0, keepdims=True), jnp.sum(index, axis=0, keepdims=True)]
    )
    well_send0[...] = jnp.concatenate([share + rate_row, sums], axis=1)
    clear_halos(0)
    clear_halos(1)
    for load in loads[6:9]:
        load.wait()
    stage_halos(0)
    for load in loads[9:]:
        load.wait()
    lines_loaded(face_block, rest_sem.at[0]).wait()
    face_coefficients()
    lateral_sum()
    interior_face(0)
    pl.semaphore_wait(barrier, len(peers))
    for dl, step in peers:
        well_copy(0, dl, step).start()
    on_sides(lambda side: halo_copy(0, side).start())
    x_copy(0).start()
    lines_loaded(other_blocks, rest_sem.at[1]).wait()
    own[3 * depth : 4 * depth, :] = gather([(inv, phi * block, width_x, depth)], slots)[0]
    slot_copy.start()

    @pl.when(me_l == 1)
    def _():
        kappa_copy.start()
        kappa[...] = jnp.zeros(kappa.shape, F32)

    for j, value in enumerate(gather([(inv, j * width_x, block, depth) for j in range(depth)], 16)):
        lines[j] = value

    for side, x in enumerate(ends_x):
        for j in range(depth):
            gain_x[side, j : j + 1, :] = whole(inv, pl.ds((phi * depth + j) * width_x + x, 1))
    for side, y in enumerate(ends_y):
        n = y // LANES
        face = packed_columns(
            [(inv.at[n], dyn_sheet(phi * depth + j)) for j in range(depth)], y - n * LANES
        )
        gain_y[side] = jnp.where(lane_x < depth, face, 0.0)
    on_sides(lambda side: halo_copy(0, side, True).wait_recv())
    edge_coefficients()
    for side in range(2):
        gain_x[side] = gain_x[side] * coef_x[side]
        edge_send[0, side] = jnp.sum(gain_x[side] * row_recv[0, side, 0], axis=0, keepdims=True)
    for side in range(2):
        gain = gain_y[side] * coef_y[side]
        gain_y[side] = gain
        edge_send[0, 2 + side, :, 0:width_x] = as_row(
            jnp.sum(gain * col_recv[0, side], axis=1, keepdims=True)
        )
    edge_pack().start()
    on_sides(lambda side: gain_copy(side).start())
    lateral_edges(0)
    solve_all()

    half = LANES // 2
    slot_copy.wait_recv()
    both = own[0 : 3 * depth, :] + pltpu.roll(par[0 : 3 * depth, :], half, 1)
    index2, at2 = both[0:depth], both[depth : 2 * depth]
    column_row, wells_row = both[2 * depth : 2 * depth + 1], both[2 * depth + 1 : 2 * depth + 2]
    wells_at = jnp.broadcast_to(wells_row, (8, LANES)).astype(jnp.int32)
    column_col = as_column(column_row)
    same = jnp.where(column_col == column_row, 1.0, 0.0).astype(BF16)

    def x_of(column):
        return jnp.floor((column + 0.5) * (1.0 / width_y))

    y_col = column_col - x_of(column_col) * width_y
    hot_y = jnp.where(
        lax.broadcasted_iota(jnp.int32, (LANES, width_y), 1).astype(F32) == y_col, 1.0, 0.0
    ).astype(BF16)
    hot_y = jnp.concatenate([hot_y, hot_y], axis=0)
    in_x = lax.broadcasted_iota(jnp.int32, (width_x, LANES), 0).astype(F32) == x_of(column_row)
    lower_half = lane < half
    face_par = pltpu.roll(par[3 * depth : 4 * depth, :], half, 1)

    def well_totals(it):
        send, recv = ((well_send0, well_recv0), (well_send1, well_recv1))[it]
        all_wells(it).wait_recv()
        mine, other = send[...], recv[tiles - 1]
        for step in range(1, tiles):
            mine, other = mine + recv[step - 1], other + recv[tiles + step - 1]
        return mine, other

    def flows(mine, other, at_slots):
        def at_wells(row):
            return jnp.take_along_axis(
                jnp.broadcast_to(row, (8, LANES)), wells_at, axis=1, mode="promise_in_bounds"
            )

        hole = jnp.where(lower_half, at_wells(mine), at_wells(other))
        return index2 * (hole - at_slots)

    def responses(flow, kappa_gain):
        change = jnp.zeros((depth, LANES), F32)
        for j in range(depth):
            change = change + lines[j] * flow[j : j + 1, :]
        out = jnp.sum(jnp.where(sub == phi, change, 0.0), axis=0, keepdims=True)
        theirs = jnp.sum(face_par * flow, axis=0, keepdims=True)
        return change, kappa_gain * out + theirs

    def spread_out(change, data):
        for i in range(depth + 1):
            row = change[i : i + 1, :] if i < depth else data
            left[sheet(i), :] = jnp.concatenate(
                [jnp.where(in_x, part, 0.0).astype(BF16) for part in split(row, 2)], axis=1
            )
        spread[...] = jnp.dot(left[...], hot_y, preferred_element_type=F32)

    @pl.when(upper_group)
    def _():
        kappa_copy.wait_recv()

    solved_at, kappa_at = gather([(solved, 0, width_x, depth), (kappa, 0, 1, 1)], slots)
    kappa_gain = jnp.where(upper_group & lower_half[0:1], kappa_at - 1.0, 0.0)
    mine, other = well_totals(0)
    index_mine, index_other = mine[:, wells:] + 1.0, other[:, wells:] + 1.0
    flow = flows(mine[:, :wells] / index_mine, other[:, :wells] / index_other, at2)
    change, data = responses(flow, kappa_gain)
    spread_out(change, data)
    x_copy(0).wait_recv()
    edge_pack().wait_recv()
    robin_data(0)
    data_at = gather([(lower_at, 0, 1, 1)], slots)[0]
    stack = jnp.concatenate([change, jnp.broadcast_to(data, (8, LANES))], axis=0)
    pile = jnp.concatenate(split(stack, 3), axis=0).astype(BF16)
    summed = jnp.dot(pile, same, preferred_element_type=F32)
    summed = (summed[0:16] + summed[16:32]) + summed[32:48]
    at_own = (solved_at + summed[0:8]) + lines[phi] * (data_at + summed[8:9])
    at_send[...] = at_own
    (share,) = binned([jnp.sum(index * at_own, axis=0, keepdims=True)])
    well_send1[...] = share + rate_row
    for dl, step in peers:
        well_copy(1, dl, step).start()
    at_copy.start()
    update()

    lateral_sum()
    interior_face(1)
    x_copy(1).start()
    stage_halos(1)
    on_sides(lambda side: halo_copy(1, side).start())
    on_sides(lambda side: gain_copy(side, True).wait_recv())
    for side in range(4):

        @pl.when(sides[side][3])
        def _():
            if side < 2:
                edge_send[1, side] = jnp.sum(
                    gain_xr[side] * row_send[1, side, 0], axis=0, keepdims=True
                )
            else:
                edge_send[1, side, :, 0:width_x] = as_row(
                    jnp.sum(gain_yr[side - 2] * col_send[1, side - 2], axis=1, keepdims=True)
                )
            edge_copy(side).start()

    on_sides(lambda side: halo_copy(1, side, True).wait_recv())
    lateral_edges(1)
    solve_all()
    at_copy.wait_recv()
    at2 = jnp.where(lower_half, at_own, pltpu.roll(at_recv[...], half, 1))
    mine, other = well_totals(1)
    flow = flows(mine / index_mine, other / index_other, at2)
    flow_out[...] = flow[:, 0:slots]
    spread_out(*responses(flow, kappa_gain))
    x_copy(1).wait_recv()
    on_sides(lambda side: edge_copy(side, True).wait_recv())
    robin_data(1)
    update()

    for it in range(ITERS):
        all_wells(it).wait_send()
        on_sides(lambda side: halo_copy(it, side).wait_send())
        x_copy(it).wait_send()
    on_sides(lambda side: gain_copy(side).wait_send())
    on_sides(lambda side: edge_copy(side).wait_send())
    edge_pack().wait_send()
    slot_copy.wait_send()
    at_copy.wait_send()

    @pl.when(me_l == 1)
    def _():
        kappa_copy.wait_send()


def fused_shards(arrays, dims):
    (
        pressure, source, perm_x, perm_y, line_inverse, robin_below,
        tile_count, perf_owner, perf_well, perf_column, perf_index, well_rate,
    ) = arrays
    groups, n_gx, n_gy = dims
    depth, width_x, width_y = pressure.shape
    tiles = n_gx * n_gy
    slots = perf_well.shape[1]
    own_wells = well_rate.shape[1]
    wells = tiles * own_wells
    sheet = (width_x, width_y)
    stack = (depth * width_x, width_y)
    halves = width_y // LANES
    HBM = pl.BlockSpec(memory_space=pltpu.HBM)
    VMEM = pl.BlockSpec(memory_space=pltpu.VMEM)
    anywhere = pl.BlockSpec(memory_space=pl.ANY)
    dma = pltpu.SemaphoreType.DMA
    i32 = jnp.int32

    def vmem(*shape):
        return pltpu.VMEM(shape, F32)

    call = pl.pallas_call(
        functools.partial(fused, (groups, n_gx, n_gy, depth)),
        out_shape=(jax.ShapeDtypeStruct(stack, F32), jax.ShapeDtypeStruct((depth, slots), F32)),
        in_specs=[HBM] * 12,
        out_specs=(VMEM, VMEM),
        scratch_shapes=[
            vmem(*stack),
            vmem(*stack),
            vmem(*stack),
            vmem(halves, depth * depth * width_x, LANES),
            vmem(*sheet),
            pltpu.SMEM((1, slots), i32),
            pltpu.VMEM((1, 1), i32),
            pltpu.VMEM((1, slots), i32),
            pltpu.VMEM((1, slots), i32),
            pltpu.VMEM((1, slots), i32),
            vmem(depth, slots),
            vmem(1, own_wells),
            vmem(halves, depth * width_x, LANES),
            vmem(halves, width_x, LANES),
            vmem(*stack),
            vmem(halves, depth * width_x, LANES),
            vmem((depth + 1) * width_x, width_y),
            pltpu.VMEM(((depth + 1) * width_x, 2 * LANES), BF16),
            vmem(4 * depth, LANES),
            vmem(4 * depth, LANES),
            vmem(depth, depth, LANES),
            vmem(depth, LANES),
            vmem(depth, LANES),
            vmem(2, depth, width_y),
            vmem(2, width_x, LANES),
            vmem(1, 2 * wells),
            vmem(groups * tiles - 1, 1, 2 * wells),
            vmem(1, wells),
            vmem(groups * tiles - 1, 1, wells),
            vmem(ITERS, 2, 2, depth, width_y),
            vmem(ITERS, 2, 2, depth, width_y),
            vmem(ITERS, 2, width_x, LANES),
            vmem(ITERS, 2, width_x, LANES),
            vmem(2, depth, width_y),
            vmem(2, width_x, LANES),
            vmem(2, depth, width_y),
            vmem(2, width_x, LANES),
            vmem(ITERS, 4, 1, width_y),
            vmem(ITERS, 4, 1, width_y),
            vmem(ITERS, *sheet),
            vmem(ITERS, *sheet),
            vmem(halves, width_x, LANES),
            dma,
            dma,
            dma((11,)),
            dma((2,)),
            dma((ITERS,)),
            dma((ITERS,)),
            dma((ITERS, 4)),
            dma((ITERS, 4)),
            dma((4,)),
            dma((4,)),
            dma((5,)),
            dma((5,)),
            dma((ITERS,)),
            dma((ITERS,)),
            dma((3,)),
            dma((3,)),
        ],
        compiler_params=pltpu.CompilerParams(
            collective_id=0, has_side_effects=True, vmem_limit_bytes=LIMIT
        ),
        name="window",
    )
    operands = (
        pressure.reshape(stack),
        source.reshape(stack),
        perm_x.reshape(stack),
        perm_y.reshape(stack),
        line_inverse.reshape(depth * depth * width_x, width_y),
        robin_below[0],
        tile_count,
        perf_owner[:, :, 0],
        perf_well,
        perf_column,
        perf_index[0].T,
        well_rate,
    )
    field, flow = call(
        *[x if x.size == 1 else pltpu.with_memory_space_constraint(x, pltpu.HBM) for x in operands]
    )
    field, flow = pl.pallas_call(
        keep,
        out_shape=(
            jax.ShapeDtypeStruct(field.shape, F32),
            jax.ShapeDtypeStruct(flow.shape, F32),
        ),
        in_specs=[anywhere] * 2,
        out_specs=(HBM, HBM),
        scratch_shapes=[dma((2,))],
        compiler_params=pltpu.CompilerParams(vmem_limit_bytes=1 << 20),
        name="keep",
    )(field, flow)
    return field.reshape(pressure.shape), flow.T[None]


def shards(
    pressure,
    source,
    perm_x,
    perm_y,
    line_inverse,
    robin_below,
    tile_count,
    perf_owner,
    perf_well,
    perf_column,
    perf_index,
    well_rate,
):
    depth, width_x, width_y = pressure.shape
    groups, n_gx, n_gy = (lax.axis_size(a) for a in ("layer", "gx", "gy"))
    tiles = n_gx * n_gy
    slots = perf_well.shape[1]
    own_wells = well_rate.shape[1]
    wells = tiles * own_wells
    powers = all(n == 1 << (n.bit_length() - 1) for n in (n_gx, n_gy))
    if (
        groups == 2
        and depth == 8
        and wells == LANES
        and slots <= LANES // 2
        and slots % 16 == 0
        and width_x <= LANES
        and width_y % LANES == 0
        and powers
    ):
        arrays = (
            pressure, source, perm_x, perm_y, line_inverse, robin_below,
            tile_count, perf_owner, perf_well, perf_column, perf_index, well_rate,
        )
        return fused_shards(arrays, (groups, n_gx, n_gy))
    sheet = (width_x, width_y)
    coefs = 1 if groups == 2 else 3
    HBM = pl.BlockSpec(memory_space=pltpu.HBM)
    anywhere = pl.BlockSpec(memory_space=pl.ANY)
    dma = pltpu.SemaphoreType.DMA
    i32 = jnp.int32
    call = pl.pallas_call(
        functools.partial(kernel, (groups, n_gx, n_gy)),
        out_shape=(
            jax.ShapeDtypeStruct(pressure.shape, F32),
            jax.ShapeDtypeStruct((depth, slots), F32),
        ),
        in_specs=[HBM] * 12,
        out_specs=(anywhere, anywhere),
        scratch_shapes=[
            pltpu.VMEM(pressure.shape, F32),
            pltpu.VMEM(pressure.shape, F32),
            pltpu.VMEM(pressure.shape, F32),
            pltpu.VMEM(pressure.shape, F32),
            pltpu.VMEM((depth, depth) + sheet, F32),
            pltpu.VMEM(sheet, F32),
            pltpu.VMEM((1, 1), i32),
            pltpu.VMEM((1, slots), i32),
            pltpu.VMEM((1, slots), i32),
            pltpu.VMEM((1, slots), i32),
            pltpu.VMEM((depth, slots), F32),
            pltpu.VMEM((1, own_wells), F32),
            pltpu.VMEM(sheet, F32),
            pltpu.VMEM(pressure.shape, F32),
            pltpu.VMEM(pressure.shape, F32),
            pltpu.VMEM((depth, slots), F32),
            pltpu.VMEM((depth, width_y), F32),
            pltpu.VMEM((width_x, 128), F32),
            pltpu.VMEM((1, 2 * wells), F32),
            pltpu.VMEM((tiles, 1, 2 * wells), F32),
            pltpu.VMEM((1, wells), F32),
            pltpu.VMEM((tiles, 1, wells), F32),
            pltpu.VMEM((ITERS, 2, 2, depth, width_y), F32),
            pltpu.VMEM((ITERS, 2, 2, depth, width_y), F32),
            pltpu.VMEM((ITERS, 2, width_x, 128), F32),
            pltpu.VMEM((ITERS, 2, width_x, 128), F32),
            pltpu.VMEM((groups, coefs) + sheet, F32),
            pltpu.VMEM((ITERS,) + sheet, F32),
            pltpu.VMEM((ITERS, groups) + sheet, F32),
            pltpu.VMEM((ITERS,) + sheet, F32),
            pltpu.VMEM((ITERS, groups) + sheet, F32),
            pltpu.VMEM(sheet, F32),
            pltpu.VMEM((groups, 1, slots), i32),
            pltpu.VMEM((ITERS, 2, slots), F32),
            pltpu.VMEM((ITERS, groups, 2, slots), F32),
            dma((12,)),
            dma((2,)),
            dma((ITERS, tiles)),
            dma((ITERS, tiles)),
            dma((ITERS, 4)),
            dma((ITERS, 4)),
            dma((groups, coefs)),
            dma((groups, coefs)),
            dma((ITERS, groups)),
            dma((ITERS, groups)),
            dma((ITERS, groups)),
            dma((ITERS, groups)),
            dma((groups,)),
            dma((groups,)),
            dma((ITERS, groups)),
            dma((ITERS, groups)),
        ],
        compiler_params=pltpu.CompilerParams(collective_id=0, has_side_effects=True, vmem_limit_bytes=LIMIT),
        name="window",
    )
    operands = (
        pressure,
        source,
        perm_x,
        perm_y,
        line_inverse[0],
        robin_below[0],
        tile_count,
        perf_owner[:, :, 0],
        perf_well,
        perf_column,
        perf_index[0].T,
        well_rate,
    )
    field, flow = call(
        *[x if x.size == 1 else pltpu.with_memory_space_constraint(x, pltpu.HBM) for x in operands]
    )
    field, flow = pl.pallas_call(
        keep,
        out_shape=(
            jax.ShapeDtypeStruct(field.shape, F32),
            jax.ShapeDtypeStruct(flow.shape, F32),
        ),
        in_specs=[anywhere] * 2,
        out_specs=(HBM, HBM),
        scratch_shapes=[dma((2,))],
        compiler_params=pltpu.CompilerParams(vmem_limit_bytes=1 << 20),
        name="keep",
    )(field, flow)
    return field, flow.T[None]


def solution(mesh):
    placed = (
        P("layer", "gx", "gy"),
        P("layer", "gx", "gy"),
        P("layer", "gx", "gy"),
        P("layer", "gx", "gy"),
        P("layer", None, None, "gx", "gy"),
        P("layer", "gx", "gy"),
        P("layer", ("gx", "gy")),
        P("layer", ("gx", "gy"), None),
        P("layer", ("gx", "gy")),
        P("layer", ("gx", "gy")),
        P("layer", ("gx", "gy"), None),
        P("layer", ("gx", "gy")),
    )
    return jax.shard_map(
        shards,
        mesh=mesh,
        in_specs=placed,
        out_specs=(P("layer", "gx", "gy"), P("layer", ("gx", "gy"), None)),
        check_vma=False,
    )
```

profile of v0, /device:TPU:0, one launch (start us, length us, event | category | flops | bytes accessed | tf_op | source)
XLA Modules:
  0.0 21.2 jit_solution(4057540688640188606)
XLA Ops:
  1.3 19.1 %window.1 = (f32[512,256]{1,0:T(8,128)S(1)}, f32[8,48]{1,0:T(8,128)S(1)}) custom-call(f32[512,256]{1,0:T(8,128)} %bitcast.15, f32[512,256]{1,0:T(8,128)} %bitcast.16, f32[512,256]{1,0:T(8,128)} %bitcast.17, f32[512,256]{1,0:T(8,128)} %bitcast.18, f32[4096,256]{1,0:T(8,128)} %bitcast.14, f32[64,256]{1,0:T(8,128)} %bitcast.19, s32[1,1]{1,0:T(1,128)S(6)} %copy.14.count_in, ...), custom_call_target="tpu_custom_call" | custom-call | tf_op jit(solution)/shard_map/window/pallas_call | solution.py:1360
  20.3 0.8 %keep.1 = (f32[512,256]{1,0:T(8,128)}, f32[8,48]{1,0:T(8,128)}) custom-call(f32[512,256]{1,0:T(8,128)S(1)} %get-tuple-element.6.field_in, f32[8,48]{1,0:T(8,128)S(1)} %get-tuple-element.7.flow_in), custom_call_target="tpu_custom_call" | custom-call | tf_op jit(solution)/shard_map/keep/pallas_call | solution.py:1363
where the time goes:
time: 21.3 us; the launch traced here: 21.2 us
  Pallas kernels  19.9 us (93%)
  between operations  1.29 us (6%)
    pallas_call x1, Pallas kernels, fused_shards(): call(*[x if x.size == 1 else pltpu.with_memory_space_constraint(x, pltpu....  19.1 us
    pallas_call x1, Pallas kernels, fused_shards(): pl.pallas_call(keep, out_shape=(jax.ShapeDtypeStruct(field.shape, F32), j...  0.81 us

commit v1 on v0

--- a/solution.py
+++ b/solution.py
@@ -1,4 +1,5 @@
 import functools
+import math
 
 import jax
 import jax.numpy as jnp
@@ -638,9 +639,8 @@
     rate_in,
     field,
     flow_out,
-    src,
-    kx,
-    ky,
+    start_at,
+    rock,
     inv,
     lower,
     column_s,
@@ -651,6 +651,7 @@
     index_v,
     rate_v,
     slabs,
+    face_lines,
     lower_at,
     rhs,
     solved,
@@ -677,24 +678,23 @@
     gain_yr,
     edge_send,
     edge_recv,
+    edge_tile,
+    edge_tile_in,
     x_send,
     x_recv,
     kappa,
     smem_sem,
-    slab_sem,
     load_sem,
     rest_sem,
     well_ssem,
     well_rsem,
-    halo_ssem,
+    side_ssem,
     halo_rsem,
-    gain_ssem,
     gain_rsem,
-    edge_ssem,
     edge_rsem,
-    x_ssem,
+    part_ssem,
     x_rsem,
-    misc_ssem,
+    kappa_ssem,
     misc_rsem,
 ):
     groups, n_gx, n_gy, depth = dims
@@ -739,20 +739,19 @@
                 (index_in, index_v),
                 (count_in, count_v),
                 (rate_in, rate_v),
-                (pressure, field),
-                (perm_x, kx),
-                (perm_y, ky),
-                (source, src),
                 (robin, lower),
             ]
         )
     ]
-    tiled = [
-        pltpu.make_async_copy(pressure.at[:, n * LANES : (n + 1) * LANES], slabs.at[n], slab_sem)
-        for n in range(halves)
+    start_load = pltpu.make_async_copy(pressure, start_at, load_sem.at[7])
+    rocks = [
+        pltpu.make_async_copy(a, rock.at[n], load_sem.at[8])
+        for n, a in enumerate((perm_x, perm_y, source))
     ]
+    rock_loaded = pltpu.make_async_copy(rock, rock, load_sem.at[8])
+    rock_x, rock_y, src = rock.at[0], rock.at[1], rock.at[2]
     barrier = pltpu.get_barrier_semaphore()
-    for load in loads[:6] + tiled:
+    for load in loads[:6] + [start_load]:
         load.start()
     for dl, step in peers:
         pl.semaphore_signal(barrier, inc=1, device_id=peer(dl, step), device_id_type=MESH)
@@ -770,7 +769,7 @@
     def lines_loaded(rows, sem):
         return pltpu.make_async_copy(inv.at[:, rows, :], inv.at[:, rows, :], sem)
 
-    for load in loads[6:] + line_loads(face_block, rest_sem.at[0]):
+    for load in rocks + line_loads(face_block, rest_sem.at[0]) + loads[6:]:
         load.start()
 
     lane = lax.broadcasted_iota(jnp.int32, (8, LANES), 1)
@@ -873,7 +872,7 @@
             a, b = row_send.at[it, at, width], row_recv.at[it, to, width]
         else:
             a, b = col_send.at[it, at - 2], col_recv.at[it, to - 2]
-        return remote(a, b, halo_ssem.at[it, at], halo_rsem.at[it, to], across(side))
+        return remote(a, b, side_ssem.at[at], halo_rsem.at[it, to], across(side))
 
     def gain_copy(side, landing=False):
         other = side ^ 1
@@ -882,25 +881,25 @@
             a, b = gain_x.at[at], gain_xr.at[to]
         else:
             a, b = gain_y.at[at - 2], gain_yr.at[to - 2]
-        return remote(a, b, gain_ssem.at[at], gain_rsem.at[to], across(side))
+        return remote(a, b, side_ssem.at[at], gain_rsem.at[to], across(side))
 
     def edge_copy(side, landing=False):
         other = side ^ 1
         at, to = (other, side) if landing else (side, other)
         return remote(
-            edge_send.at[1, at], edge_recv.at[1, to], edge_ssem.at[at], edge_rsem.at[to],
+            edge_send.at[at], edge_recv.at[to], side_ssem.at[at], edge_rsem.at[to],
             across(side, True),
         )
 
     def edge_pack():
-        return remote(edge_send.at[0], edge_recv.at[0], edge_ssem.at[4], edge_rsem.at[4], partner)
+        return remote(edge_tile, edge_tile_in, part_ssem, edge_rsem.at[4], partner)
 
     def x_copy(it):
-        return remote(x_send.at[it], x_recv.at[it], x_ssem.at[it], x_rsem.at[it], partner)
-
-    slot_copy = remote(own, par, misc_ssem.at[0], misc_rsem.at[0], partner)
-    at_copy = remote(at_send, at_recv, misc_ssem.at[1], misc_rsem.at[1], partner)
-    kappa_copy = remote(inv.at[:, 0:width_x, :], kappa, misc_ssem.at[2], misc_rsem.at[2], partner)
+        return remote(x_send.at[it], x_recv.at[it], part_ssem, x_rsem.at[it], partner)
+
+    slot_copy = remote(own, par, part_ssem, misc_rsem.at[0], partner)
+    at_copy = remote(at_send, at_recv, part_ssem, misc_rsem.at[1], partner)
+    kappa_copy = remote(inv.at[:, 0:width_x, :], kappa, kappa_ssem, misc_rsem.at[2], partner)
 
     lane_x = lax.broadcasted_iota(jnp.int32, (width_x, LANES), 1)
 
@@ -921,10 +920,10 @@
         for side, x in enumerate(ends_x):
             for l in range(depth):
                 row = l * width_x + x
-                row_send[it, side, 0, l : l + 1, :] = field[row : row + 1, :]
+                row_send[it, side, 0, l : l + 1, :] = (field if it else start_at)[row : row + 1, :]
                 if it == 0:
-                    row_send[it, side, 1, l : l + 1, :] = kx[row : row + 1, :]
-        blocks = each(field) + (each(ky) if it == 0 else [])
+                    row_send[it, side, 1, l : l + 1, :] = rock_x[row : row + 1, :]
+        blocks = each(field) if it else each(start_at) + each(rock_y)
         for side, y in enumerate(ends_y):
             col_send[it, side] = packed_columns(blocks, y)
 
@@ -938,7 +937,7 @@
                 else:
                     col_recv[it, side - 2] = jnp.zeros(col_recv.shape[2:], F32)
                 if it == 1:
-                    edge_recv[it, side] = jnp.zeros(edge_recv.shape[2:], F32)
+                    edge_recv[side] = jnp.zeros(edge_recv.shape[1:], F32)
 
     def on_sides(body):
         for side in range(4):
@@ -949,15 +948,15 @@
 
     def face_coefficients():
         for l in range(depth):
-            mult = kx[sheet(l), :]
-            kx[sheet(l), :] = jnp.where(first_x, 0.0, 0.5 * (mult + pltpu.roll(mult, width_x - 1, 0)))
-            mult = ky[sheet(l), :]
-            ky[sheet(l), :] = jnp.where(first_y, 0.0, 0.5 * (mult + pltpu.roll(mult, width_y - 1, 1)))
-
-    def lateral_sum():
+            mult = rock_x[sheet(l), :]
+            rock_x[sheet(l), :] = jnp.where(first_x, 0.0, 0.5 * (mult + pltpu.roll(mult, width_x - 1, 0)))
+            mult = rock_y[sheet(l), :]
+            rock_y[sheet(l), :] = jnp.where(first_y, 0.0, 0.5 * (mult + pltpu.roll(mult, width_y - 1, 1)))
+
+    def lateral_sum(now_at):
         for l in range(depth):
-            now = field[sheet(l), :]
-            face_x, face_y = kx[sheet(l), :], ky[sheet(l), :]
+            now = now_at[sheet(l), :]
+            face_x, face_y = rock_x[sheet(l), :], rock_y[sheet(l), :]
             east = face_x * pltpu.roll(now, width_x - 1, 0)
             west = pltpu.roll(face_x * now, 1, 0)
             north = face_y * pltpu.roll(now, width_y - 1, 1)
@@ -985,11 +984,15 @@
             )
 
     def chunk_loop(body):
+        chunks = width_x // ROWS
+        together = math.gcd(chunks, 4)
+
         def step(c, carry):
-            body(pl.multiple_of(c * ROWS, ROWS))
+            for k in range(together):
+                body(pl.multiple_of((c * together + k) * ROWS, ROWS))
             return carry
 
-        lax.fori_loop(0, width_x // ROWS, step, 0)
+        lax.fori_loop(0, chunks // together, step, 0)
 
     def whole(ref, rows):
         return jnp.concatenate([ref[n, rows, :] for n in range(halves)], axis=1)
@@ -1023,43 +1026,35 @@
 
         chunk_loop(body)
 
-    def robin_data(it):
-        for side, x in enumerate(ends_x):
-            x_recv[it, x : x + 1, :] += edge_recv[it, side]
-        for side, y in enumerate(ends_y):
-            x_recv[it, :, y : y + 1] += as_column(edge_recv[it, 2 + side, :, 0:width_x])
-
+    def inner_face(it, at):
+        mine = whole(solved, rows_of(phi, at)) + own_face(at)
+        return x_recv[it, pl.ds(at, ROWS), :] + jnp.where(
+            upper_group, whole(kappa, pl.ds(at, ROWS)) * mine - mine, 0.0
+        )
+
+    def interior_data(it):
         def body(at):
-            rows = pl.ds(at, ROWS)
-            mine = whole(solved, rows_of(phi, at)) + own_face(at)
-            data = x_recv[it, rows, :] + jnp.where(upper_group, whole(kappa, rows) * mine - mine, 0.0)
-            lower[rows, :] = data
-            for n in range(halves):
-                lower_at[n, rows, :] = data[:, n * LANES : (n + 1) * LANES]
+            data = inner_face(it, at)
+            lower[pl.ds(at, ROWS), :] = data
+            for n in range(halves if it == 0 else 0):
+                lower_at[n, pl.ds(at, ROWS), :] = data[:, n * LANES : (n + 1) * LANES]
 
         chunk_loop(body)
 
-    def update():
-        def body(at):
-            rows = pl.ds(at, ROWS)
-            data = lower[rows, :] + spread[rows_of(depth, at), :]
-            lower[rows, :] = data
-            for i in range(depth):
-                field[rows_of(i, at), :] = (
-                    whole(solved, rows_of(i, at))
-                    + spread[rows_of(i, at), :]
-                    + whole(inv, rows_of(i * depth + phi, at)) * data
-                )
-
-        chunk_loop(body)
-
-    def start(copy):
-        copy.start()
+    def add_edges(ref, rows, columns):
+        for x, row in zip(ends_x, rows):
+            ref[x : x + 1, :] += row
+        for y, column in zip(ends_y, columns):
+            tile = y - y % LANES
+            column = as_column(column)
+            ref[:, tile : tile + LANES] += jnp.where(lane_x == y - tile, column, 0.0)
 
     to_smem.wait()
-    pltpu.make_async_copy(slabs, slabs, slab_sem).wait()
+    start_load.wait()
     for load in line_loads(other_blocks, rest_sem.at[1]):
         load.start()
+    for n in range(halves):
+        slabs[n] = start_at[:, n * LANES : (n + 1) * LANES]
     at_own = gather([(slabs, 0, width_x, depth)], slots)[0]
     own[depth : 2 * depth, :] = at_own
     share, sums = binned(
@@ -1068,31 +1063,28 @@
     well_send0[...] = jnp.concatenate([share + rate_row, sums], axis=1)
     clear_halos(0)
     clear_halos(1)
-    for load in loads[6:9]:
-        load.wait()
+    rock_loaded.wait()
     stage_halos(0)
-    for load in loads[9:]:
-        load.wait()
+    loads[6].wait()
     lines_loaded(face_block, rest_sem.at[0]).wait()
-    face_coefficients()
-    lateral_sum()
-    interior_face(0)
+    for n in range(halves):
+        face_lines[n] = inv[n, face_block, :]
+    own[3 * depth : 4 * depth, :] = gather([(face_lines, 0, width_x, depth)], slots)[0]
     pl.semaphore_wait(barrier, len(peers))
     for dl, step in peers:
         well_copy(0, dl, step).start()
+    slot_copy.start()
     on_sides(lambda side: halo_copy(0, side).start())
-    x_copy(0).start()
-    lines_loaded(other_blocks, rest_sem.at[1]).wait()
-    own[3 * depth : 4 * depth, :] = gather([(inv, phi * block, width_x, depth)], slots)[0]
-    slot_copy.start()
 
     @pl.when(me_l == 1)
     def _():
         kappa_copy.start()
         kappa[...] = jnp.zeros(kappa.shape, F32)
 
-    for j, value in enumerate(gather([(inv, j * width_x, block, depth) for j in range(depth)], 16)):
-        lines[j] = value
+    face_coefficients()
+    lateral_sum(start_at)
+    interior_face(0)
+    x_copy(0).start()
 
     for side, x in enumerate(ends_x):
         for j in range(depth):
@@ -1103,21 +1095,34 @@
             [(inv.at[n], dyn_sheet(phi * depth + j)) for j in range(depth)], y - n * LANES
         )
         gain_y[side] = jnp.where(lane_x < depth, face, 0.0)
+    lines_loaded(other_blocks, rest_sem.at[1]).wait()
+
+    def gather_lines(columns):
+        found = gather([(inv, j * width_x, block, depth) for j in columns], 16)
+        for j, value in zip(columns, found):
+            lines[j] = value
+
+    gather_lines(range(depth - 2))
+    edge_tile[...] = jnp.zeros(edge_tile.shape, F32)
     on_sides(lambda side: halo_copy(0, side, True).wait_recv())
     edge_coefficients()
     for side in range(2):
         gain_x[side] = gain_x[side] * coef_x[side]
-        edge_send[0, side] = jnp.sum(gain_x[side] * row_recv[0, side, 0], axis=0, keepdims=True)
+        edge = jnp.sum(gain_x[side] * row_recv[0, side, 0], axis=0, keepdims=True)
+        for n in range(halves):
+            edge_tile[side * halves + n : side * halves + n + 1, :] = edge[:, n * LANES : (n + 1) * LANES]
     for side in range(2):
         gain = gain_y[side] * coef_y[side]
         gain_y[side] = gain
-        edge_send[0, 2 + side, :, 0:width_x] = as_row(
+        row = 2 * halves + side
+        edge_tile[row : row + 1, 0:width_x] = as_row(
             jnp.sum(gain * col_recv[0, side], axis=1, keepdims=True)
         )
     edge_pack().start()
-    on_sides(lambda side: gain_copy(side).start())
+    gather_lines(range(depth - 2, depth))
     lateral_edges(0)
     solve_all()
+    on_sides(lambda side: gain_copy(side).start())
 
     half = LANES // 2
     slot_copy.wait_recv()
@@ -1138,6 +1143,18 @@
     hot_y = jnp.concatenate([hot_y, hot_y], axis=0)
     in_x = lax.broadcasted_iota(jnp.int32, (width_x, LANES), 0).astype(F32) == x_of(column_row)
     lower_half = lane < half
+    x_row = x_of(column_row)
+    y_row = column_row - x_row * width_y
+    x_all, y_all = (jnp.broadcast_to(v, (8, LANES)).astype(jnp.int32) for v in (x_row, y_row))
+    edge_lanes = jnp.where(sub < 2 * halves, y_all & (LANES - 1), x_all)
+    edge_spots = jnp.zeros((8, LANES), jnp.int32)
+    for side, x in enumerate(ends_x):
+        for n in range(halves):
+            here = (x_all == x) & (y_all >= n * LANES) & (y_all < (n + 1) * LANES)
+            edge_spots = jnp.where((sub == side * halves + n) & here, 1, edge_spots)
+    for side, y in enumerate(ends_y):
+        edge_spots = jnp.where((sub == 2 * halves + side) & (y_all == y), 1, edge_spots)
+    edge_spots = edge_spots > 0
     face_par = pltpu.roll(par[3 * depth : 4 * depth, :], half, 1)
 
     def well_totals(it):
@@ -1157,37 +1174,61 @@
         hole = jnp.where(lower_half, at_wells(mine), at_wells(other))
         return index2 * (hole - at_slots)
 
-    def responses(flow, kappa_gain):
+    def responses(flow):
         change = jnp.zeros((depth, LANES), F32)
         for j in range(depth):
             change = change + lines[j] * flow[j : j + 1, :]
         out = jnp.sum(jnp.where(sub == phi, change, 0.0), axis=0, keepdims=True)
         theirs = jnp.sum(face_par * flow, axis=0, keepdims=True)
-        return change, kappa_gain * out + theirs
+        return change, out, theirs
 
     def spread_out(change, data):
-        for i in range(depth + 1):
-            row = change[i : i + 1, :] if i < depth else data
-            left[sheet(i), :] = jnp.concatenate(
-                [jnp.where(in_x, part, 0.0).astype(BF16) for part in split(row, 2)], axis=1
+        order = [depth] + list(range(depth))
+        for first in range(0, depth + 1, 3):
+            some = order[first : first + 3]
+            rows = slice(first * width_x, (first + len(some)) * width_x)
+            for n, i in enumerate(some):
+                row = change[i : i + 1, :] if i < depth else data
+                left[sheet(first + n), :] = jnp.concatenate(
+                    [jnp.where(in_x, part, 0.0).astype(BF16) for part in split(row, 2)], axis=1
+                )
+            spread[rows, :] = jnp.dot(left[rows, :], hot_y, preferred_element_type=F32)
+
+    def update():
+        lower[...] = lower[...] + spread[sheet(0), :]
+        for i in range(depth):
+            field[sheet(i), :] = (
+                whole(solved, sheet(i))
+                + spread[sheet(i + 1), :]
+                + whole(inv, dyn_sheet(i * depth + phi)) * lower[...]
             )
-        spread[...] = jnp.dot(left[...], hot_y, preferred_element_type=F32)
+
+    (solved_at,) = gather([(solved, 0, width_x, depth)], slots)
+    mine, other = well_totals(0)
+    index_mine, index_other = mine[:, wells:] + 1.0, other[:, wells:] + 1.0
+    flow = flows(mine[:, :wells] / index_mine, other[:, :wells] / index_other, at2)
+    change, out, theirs = responses(flow)
 
     @pl.when(upper_group)
     def _():
         kappa_copy.wait_recv()
 
-    solved_at, kappa_at = gather([(solved, 0, width_x, depth), (kappa, 0, 1, 1)], slots)
+    x_copy(0).wait_recv()
+    interior_data(0)
+    data_at, kappa_at = gather([(lower_at, 0, 1, 1), (kappa, 0, 1, 1)], slots)
     kappa_gain = jnp.where(upper_group & lower_half[0:1], kappa_at - 1.0, 0.0)
-    mine, other = well_totals(0)
-    index_mine, index_other = mine[:, wells:] + 1.0, other[:, wells:] + 1.0
-    flow = flows(mine[:, :wells] / index_mine, other[:, :wells] / index_other, at2)
-    change, data = responses(flow, kappa_gain)
-    spread_out(change, data)
-    x_copy(0).wait_recv()
+    data = kappa_gain * out + theirs
     edge_pack().wait_recv()
-    robin_data(0)
-    data_at = gather([(lower_at, 0, 1, 1)], slots)[0]
+    edges = edge_tile_in[...]
+    data_at = data_at + jnp.sum(
+        jnp.where(
+            edge_spots,
+            jnp.take_along_axis(edges, edge_lanes, axis=1, mode="promise_in_bounds"),
+            0.0,
+        ),
+        axis=0,
+        keepdims=True,
+    )
     stack = jnp.concatenate([change, jnp.broadcast_to(data, (8, LANES))], axis=0)
     pile = jnp.concatenate(split(stack, 3), axis=0).astype(BF16)
     summed = jnp.dot(pile, same, preferred_element_type=F32)
@@ -1199,9 +1240,18 @@
     for dl, step in peers:
         well_copy(1, dl, step).start()
     at_copy.start()
+    spread_out(change, data)
+    add_edges(
+        lower,
+        [
+            jnp.concatenate([edges[side * halves + n : side * halves + n + 1] for n in range(halves)], axis=1)
+            for side in range(2)
+        ],
+        [edges[2 * halves + side : 2 * halves + side + 1, 0:width_x] for side in range(2)],
+    )
     update()
 
-    lateral_sum()
+    lateral_sum(field)
     interior_face(1)
     x_copy(1).start()
     stage_halos(1)
@@ -1212,11 +1262,11 @@
         @pl.when(sides[side][3])
         def _():
             if side < 2:
-                edge_send[1, side] = jnp.sum(
-                    gain_xr[side] * row_send[1, side, 0], axis=0, keepdims=True
-                )
+                edge = jnp.sum(gain_xr[side] * row_send[1, side, 0], axis=0, keepdims=True)
+                for n in range(halves):
+                    edge_send[side, n : n + 1, :] = edge[:, n * LANES : (n + 1) * LANES]
             else:
-                edge_send[1, side, :, 0:width_x] = as_row(
+                edge_send[side, 0:1, 0:width_x] = as_row(
                     jnp.sum(gain_yr[side - 2] * col_send[1, side - 2], axis=1, keepdims=True)
                 )
             edge_copy(side).start()
@@ -1229,21 +1279,37 @@
     mine, other = well_totals(1)
     flow = flows(mine / index_mine, other / index_other, at2)
     flow_out[...] = flow[:, 0:slots]
-    spread_out(*responses(flow, kappa_gain))
+    change, out, theirs = responses(flow)
+    spread_out(change, kappa_gain * out + theirs)
     x_copy(1).wait_recv()
     on_sides(lambda side: edge_copy(side, True).wait_recv())
-    robin_data(1)
+    add_edges(
+        x_recv.at[1],
+        [
+            jnp.concatenate([edge_recv[side, n : n + 1, :] for n in range(halves)], axis=1)
+            for side in range(2)
+        ],
+        [edge_recv[2 + side, 0:1, 0:width_x] for side in range(2)],
+    )
+    interior_data(1)
     update()
+
+    def sent(sem, buffers):
+        rows = sum(math.prod(b.shape) for b in buffers) // LANES
+        span = solved.at[0, 0:rows, :]
+        remote(span, span, sem, sem, partner).wait_send()
+
+    def side_sent(side):
+        if side < 2:
+            pieces = [row_send.at[0, 0], row_send.at[0, 0, 0], gain_x.at[0], edge_send.at[0]]
+        else:
+            pieces = [col_send.at[0, 0], col_send.at[0, 0], gain_y.at[0], edge_send.at[0]]
+        sent(side_ssem.at[side], pieces)
 
     for it in range(ITERS):
         all_wells(it).wait_send()
-        on_sides(lambda side: halo_copy(it, side).wait_send())
-        x_copy(it).wait_send()
-    on_sides(lambda side: gain_copy(side).wait_send())
-    on_sides(lambda side: edge_copy(side).wait_send())
-    edge_pack().wait_send()
-    slot_copy.wait_send()
-    at_copy.wait_send()
+    on_sides(side_sent)
+    sent(part_ssem, [own, edge_tile, at_send, x_send])
 
     @pl.when(me_l == 1)
     def _():
@@ -1280,8 +1346,7 @@
         out_specs=(VMEM, VMEM),
         scratch_shapes=[
             vmem(*stack),
-            vmem(*stack),
-            vmem(*stack),
+            vmem(3, *stack),
             vmem(halves, depth * depth * width_x, LANES),
             vmem(*sheet),
             pltpu.SMEM((1, slots), i32),
@@ -1291,6 +1356,7 @@
             pltpu.VMEM((1, slots), i32),
             vmem(depth, slots),
             vmem(1, own_wells),
+            vmem(halves, depth * width_x, LANES),
             vmem(halves, depth * width_x, LANES),
             vmem(halves, width_x, LANES),
             vmem(*stack),
@@ -1316,26 +1382,25 @@
             vmem(2, width_x, LANES),
             vmem(2, depth, width_y),
             vmem(2, width_x, LANES),
-            vmem(ITERS, 4, 1, width_y),
-            vmem(ITERS, 4, 1, width_y),
+            vmem(4, depth, LANES),
+            vmem(4, depth, LANES),
+            vmem(depth, LANES),
+            vmem(depth, LANES),
             vmem(ITERS, *sheet),
             vmem(ITERS, *sheet),
             vmem(halves, width_x, LANES),
             dma,
-            dma,
-            dma((11,)),
+            dma((9,)),
             dma((2,)),
             dma((ITERS,)),
             dma((ITERS,)),
-            dma((ITERS, 4)),
+            dma((4,)),
             dma((ITERS, 4)),
             dma((4,)),
-            dma((4,)),
             dma((5,)),
-            dma((5,)),
+            dma,
             dma((ITERS,)),
-            dma((ITERS,)),
-            dma((3,)),
+            dma,
             dma((3,)),
         ],
         compiler_params=pltpu.CompilerParams(
@@ -1404,6 +1469,7 @@
         and slots % 16 == 0
         and width_x <= LANES
         and width_y % LANES == 0
+        and 2 * (width_y // LANES) + 2 <= depth
         and powers
     ):
         arrays = (

time: 21.3 us -> 20.3 us (0.953)
  Pallas kernels: 19.9 us -> 18.8 us
    pallas_call x1, Pallas kernels: 19.1 us -> 18 us  [fused_shards(): call(*[x if x.size == 1 else pltpu.with_memory_space_constraint(x, pltpu....]
where the time goes in v1:
time: 20.3 us; the launch traced here: 20.1 us
  Pallas kernels  18.8 us (93%)
  between operations  1.29 us (6%)
    pallas_call x1, Pallas kernels, fused_shards(): call(*[x if x.size == 1 else pltpu.with_memory_space_constraint(x, pltpu....  18 us
    pallas_call x1, Pallas kernels, fused_shards(): pl.pallas_call(keep, out_shape=(jax.ShapeDtypeStruct(field.shape, F32), j...  0.81 us

profile of v1, /device:TPU:0, one launch (start us, length us, event | category | flops | bytes accessed | tf_op | source)
XLA Modules:
  0.0 20.1 jit_solution(11185067495938838018)
XLA Ops:
  1.3 18.0 %window.1 = (f32[512,256]{1,0:T(8,128)S(1)}, f32[8,48]{1,0:T(8,128)S(1)}) custom-call(f32[512,256]{1,0:T(8,128)} %bitcast.15, f32[512,256]{1,0:T(8,128)} %bitcast.16, f32[512,256]{1,0:T(8,128)} %bitcast.17, f32[512,256]{1,0:T(8,128)} %bitcast.18, f32[4096,256]{1,0:T(8,128)} %bitcast.14, f32[64,256]{1,0:T(8,128)} %bitcast.19, s32[1,1]{1,0:T(1,128)S(6)} %copy.14.count_in, ...), custom_call_target="tpu_custom_call" | custom-call | tf_op jit(solution)/shard_map/window/pallas_call | solution.py:1425
  19.3 0.8 %keep.1 = (f32[512,256]{1,0:T(8,128)}, f32[8,48]{1,0:T(8,128)}) custom-call(f32[512,256]{1,0:T(8,128)S(1)} %get-tuple-element.6.field_in, f32[8,48]{1,0:T(8,128)S(1)} %get-tuple-element.7.flow_in), custom_call_target="tpu_custom_call" | custom-call | tf_op jit(solution)/shard_map/keep/pallas_call | solution.py:1428

commit v2 on v1

--- a/solution.py
+++ b/solution.py
@@ -15,6 +15,7 @@
 BF16 = jnp.bfloat16
 ROWS = 8
 LANES = 128
+PACK = 16
 
 
 def pieces(value):
@@ -903,16 +904,36 @@
 
     lane_x = lax.broadcasted_iota(jnp.int32, (width_x, LANES), 1)
 
+    parts = width_x // ROWS
+
     def packed_columns(blocks, y):
-        out = jnp.zeros((width_x, LANES), F32)
-        for at, (ref, rows) in enumerate(blocks):
-            tile = y - y % LANES
-            value = ref[rows, tile : tile + LANES]
-            out = jnp.where(lane_x == at, pltpu.roll(value, (at - y) % LANES, 1), out)
+        out = jnp.zeros((ROWS, LANES), F32)
+        tile = y - y % LANES
+        for at, (ref, first) in enumerate(blocks):
+            for n in range(parts):
+                value = ref[pl.ds(first + n * ROWS, ROWS), tile : tile + LANES]
+                to = n * PACK + at
+                out = jnp.where(lane == to, pltpu.roll(value, (to - y) % LANES, 1), out)
         return out
 
+    entry = lax.broadcasted_iota(jnp.int32, (LANES, LANES), 0)
+    cell = lax.broadcasted_iota(jnp.int32, (LANES, LANES), 1)
+    own_entries = ((entry & (PACK - 1)) < depth) & ((entry >> (PACK.bit_length() - 1)) == (cell >> 3))
+    own_entries = jnp.where(own_entries, 1.0, 0.0).astype(BF16)
+
+    def column_sums(values):
+        pile = jnp.concatenate([part for value in values for part in split(value, 3)], axis=0)
+        total = jnp.dot(pile.astype(BF16), own_entries, preferred_element_type=F32)
+        at_row = (lane & (ROWS - 1)) == sub
+        rows = []
+        for n in range(len(values)):
+            some = [total[(3 * n + k) * ROWS : (3 * n + k + 1) * ROWS] for k in range(3)]
+            picked = jnp.where(at_row, (some[0] + some[1]) + some[2], 0.0)
+            rows.append(jnp.sum(picked, axis=0, keepdims=True)[:, 0:width_x])
+        return rows
+
     def each(ref):
-        return [(ref, sheet(l)) for l in range(depth)]
+        return [(ref, l * width_x) for l in range(depth)]
 
     ends_x, ends_y = (0, width_x - 1), (0, width_y - 1)
 
@@ -937,6 +958,10 @@
                 else:
                     col_recv[it, side - 2] = jnp.zeros(col_recv.shape[2:], F32)
                 if it == 1:
+                    if side < 2:
+                        gain_xr[side] = jnp.zeros(gain_xr.shape[1:], F32)
+                    else:
+                        gain_yr[side - 2] = jnp.zeros(gain_yr.shape[1:], F32)
                     edge_recv[side] = jnp.zeros(edge_recv.shape[1:], F32)
 
     def on_sides(body):
@@ -973,8 +998,10 @@
             tile = y - y % LANES
             terms = coef_y[side] * col_recv[it, side]
             for l in range(depth):
-                term = pltpu.roll(terms, (y - l) % LANES, 1)
-                rhs[sheet(l), tile : tile + LANES] += jnp.where(lane_x == y - tile, term, 0.0)
+                for n in range(parts):
+                    term = pltpu.roll(terms, (y - n * PACK - l) % LANES, 1)
+                    rows = slice(l * width_x + n * ROWS, l * width_x + (n + 1) * ROWS)
+                    rhs[rows, tile : tile + LANES] += jnp.where(lane == y - tile, term, 0.0)
 
     def edge_coefficients():
         for side in range(2):
@@ -1057,10 +1084,10 @@
         slabs[n] = start_at[:, n * LANES : (n + 1) * LANES]
     at_own = gather([(slabs, 0, width_x, depth)], slots)[0]
     own[depth : 2 * depth, :] = at_own
-    share, sums = binned(
+    share, index_sums = binned(
         [jnp.sum(index * at_own, axis=0, keepdims=True), jnp.sum(index, axis=0, keepdims=True)]
     )
-    well_send0[...] = jnp.concatenate([share + rate_row, sums], axis=1)
+    well_send0[...] = jnp.concatenate([share + rate_row, index_sums], axis=1)
     clear_halos(0)
     clear_halos(1)
     rock_loaded.wait()
@@ -1071,10 +1098,10 @@
         face_lines[n] = inv[n, face_block, :]
     own[3 * depth : 4 * depth, :] = gather([(face_lines, 0, width_x, depth)], slots)[0]
     pl.semaphore_wait(barrier, len(peers))
+    on_sides(lambda side: halo_copy(0, side).start())
+    slot_copy.start()
     for dl, step in peers:
         well_copy(0, dl, step).start()
-    slot_copy.start()
-    on_sides(lambda side: halo_copy(0, side).start())
 
     @pl.when(me_l == 1)
     def _():
@@ -1092,9 +1119,10 @@
     for side, y in enumerate(ends_y):
         n = y // LANES
         face = packed_columns(
-            [(inv.at[n], dyn_sheet(phi * depth + j)) for j in range(depth)], y - n * LANES
-        )
-        gain_y[side] = jnp.where(lane_x < depth, face, 0.0)
+            [(inv.at[n], pl.multiple_of((phi * depth + j) * width_x, width_x)) for j in range(depth)],
+            y - n * LANES,
+        )
+        gain_y[side] = jnp.where((lane & (PACK - 1)) < depth, face, 0.0)
     lines_loaded(other_blocks, rest_sem.at[1]).wait()
 
     def gather_lines(columns):
@@ -1111,13 +1139,11 @@
         edge = jnp.sum(gain_x[side] * row_recv[0, side, 0], axis=0, keepdims=True)
         for n in range(halves):
             edge_tile[side * halves + n : side * halves + n + 1, :] = edge[:, n * LANES : (n + 1) * LANES]
+    sums = column_sums([gain_y[side] * coef_y[side] * col_recv[0, side] for side in range(2)])
     for side in range(2):
-        gain = gain_y[side] * coef_y[side]
-        gain_y[side] = gain
+        gain_y[side] = gain_y[side] * coef_y[side]
         row = 2 * halves + side
-        edge_tile[row : row + 1, 0:width_x] = as_row(
-            jnp.sum(gain * col_recv[0, side], axis=1, keepdims=True)
-        )
+        edge_tile[row : row + 1, 0:width_x] = sums[side]
     edge_pack().start()
     gather_lines(range(depth - 2, depth))
     lateral_edges(0)
@@ -1208,6 +1234,11 @@
     index_mine, index_other = mine[:, wells:] + 1.0, other[:, wells:] + 1.0
     flow = flows(mine[:, :wells] / index_mine, other[:, :wells] / index_other, at2)
     change, out, theirs = responses(flow)
+    stack = jnp.concatenate([change, jnp.where(sub == 0, out, theirs)], axis=0)
+    pile = jnp.concatenate(split(stack, 3), axis=0).astype(BF16)
+    summed = jnp.dot(pile, same, preferred_element_type=F32)
+    summed = (summed[0:16] + summed[16:32]) + summed[32:48]
+    inner_at = lines[phi]
 
     @pl.when(upper_group)
     def _():
@@ -1218,9 +1249,12 @@
     data_at, kappa_at = gather([(lower_at, 0, 1, 1), (kappa, 0, 1, 1)], slots)
     kappa_gain = jnp.where(upper_group & lower_half[0:1], kappa_at - 1.0, 0.0)
     data = kappa_gain * out + theirs
+    at_own = (solved_at + summed[0:8]) + inner_at * (
+        data_at + (kappa_gain * summed[8:9] + summed[9:10])
+    )
     edge_pack().wait_recv()
     edges = edge_tile_in[...]
-    data_at = data_at + jnp.sum(
+    at_own = at_own + inner_at * jnp.sum(
         jnp.where(
             edge_spots,
             jnp.take_along_axis(edges, edge_lanes, axis=1, mode="promise_in_bounds"),
@@ -1229,16 +1263,11 @@
         axis=0,
         keepdims=True,
     )
-    stack = jnp.concatenate([change, jnp.broadcast_to(data, (8, LANES))], axis=0)
-    pile = jnp.concatenate(split(stack, 3), axis=0).astype(BF16)
-    summed = jnp.dot(pile, same, preferred_element_type=F32)
-    summed = (summed[0:16] + summed[16:32]) + summed[32:48]
-    at_own = (solved_at + summed[0:8]) + lines[phi] * (data_at + summed[8:9])
-    at_send[...] = at_own
     (share,) = binned([jnp.sum(index * at_own, axis=0, keepdims=True)])
     well_send1[...] = share + rate_row
     for dl, step in peers:
         well_copy(1, dl, step).start()
+    at_send[...] = at_own
     at_copy.start()
     spread_out(change, data)
     add_edges(
@@ -1251,26 +1280,20 @@
     )
     update()
 
+    stage_halos(1)
+    on_sides(lambda side: halo_copy(1, side).start())
     lateral_sum(field)
     interior_face(1)
     x_copy(1).start()
-    stage_halos(1)
-    on_sides(lambda side: halo_copy(1, side).start())
     on_sides(lambda side: gain_copy(side, True).wait_recv())
-    for side in range(4):
-
-        @pl.when(sides[side][3])
-        def _():
-            if side < 2:
-                edge = jnp.sum(gain_xr[side] * row_send[1, side, 0], axis=0, keepdims=True)
-                for n in range(halves):
-                    edge_send[side, n : n + 1, :] = edge[:, n * LANES : (n + 1) * LANES]
-            else:
-                edge_send[side, 0:1, 0:width_x] = as_row(
-                    jnp.sum(gain_yr[side - 2] * col_send[1, side - 2], axis=1, keepdims=True)
-                )
-            edge_copy(side).start()
-
+    for side in range(2):
+        edge = jnp.sum(gain_xr[side] * row_send[1, side, 0], axis=0, keepdims=True)
+        for n in range(halves):
+            edge_send[side, n : n + 1, :] = edge[:, n * LANES : (n + 1) * LANES]
+    sums = column_sums([gain_yr[side] * col_send[1, side] for side in range(2)])
+    for side in range(2):
+        edge_send[2 + side, 0:1, 0:width_x] = sums[side]
+    on_sides(lambda side: edge_copy(side).start())
     on_sides(lambda side: halo_copy(1, side, True).wait_recv())
     lateral_edges(1)
     solve_all()
@@ -1369,19 +1392,19 @@
             vmem(depth, LANES),
             vmem(depth, LANES),
             vmem(2, depth, width_y),
-            vmem(2, width_x, LANES),
+            vmem(2, ROWS, LANES),
             vmem(1, 2 * wells),
             vmem(groups * tiles - 1, 1, 2 * wells),
             vmem(1, wells),
             vmem(groups * tiles - 1, 1, wells),
             vmem(ITERS, 2, 2, depth, width_y),
             vmem(ITERS, 2, 2, depth, width_y),
-            vmem(ITERS, 2, width_x, LANES),
-            vmem(ITERS, 2, width_x, LANES),
+            vmem(ITERS, 2, ROWS, LANES),
+            vmem(ITERS, 2, ROWS, LANES),
             vmem(2, depth, width_y),
-            vmem(2, width_x, LANES),
+            vmem(2, ROWS, LANES),
             vmem(2, depth, width_y),
-            vmem(2, width_x, LANES),
+            vmem(2, ROWS, LANES),
             vmem(4, depth, LANES),
             vmem(4, depth, LANES),
             vmem(depth, LANES),
@@ -1467,7 +1490,8 @@
         and wells == LANES
         and slots <= LANES // 2
         and slots % 16 == 0
-        and width_x <= LANES
+        and width_x % ROWS == 0
+        and width_x // ROWS * PACK <= LANES
         and width_y % LANES == 0
         and 2 * (width_y // LANES) + 2 <= depth
         and powers

time: 20.3 us -> 20 us (0.985)
  Pallas kernels: 18.8 us -> 18.5 us
    pallas_call x1, Pallas kernels: 18 us -> 17.7 us  [fused_shards(): call(*[x if x.size == 1 else pltpu.with_memory_space_constraint(x, pltpu....]
where the time goes in v2:
time: 20 us; the launch traced here: 19.8 us
  Pallas kernels  18.5 us (92%)
  between operations  1.29 us (6%)
    pallas_call x1, Pallas kernels, fused_shards(): call(*[x if x.size == 1 else pltpu.with_memory_space_constraint(x, pltpu....  17.7 us
    pallas_call x1, Pallas kernels, fused_shards(): pl.pallas_call(keep, out_shape=(jax.ShapeDtypeStruct(field.shape, F32), j...  0.81 us

profile of v2, /device:TPU:0, one launch (start us, length us, event | category | flops | bytes accessed | tf_op | source)
XLA Modules:
  0.0 19.8 jit_solution(13512162524132366872)
XLA Ops:
  1.3 17.7 %window.1 = (f32[512,256]{1,0:T(8,128)S(1)}, f32[8,48]{1,0:T(8,128)S(1)}) custom-call(f32[512,256]{1,0:T(8,128)} %bitcast.15, f32[512,256]{1,0:T(8,128)} %bitcast.16, f32[512,256]{1,0:T(8,128)} %bitcast.17, f32[512,256]{1,0:T(8,128)} %bitcast.18, f32[4096,256]{1,0:T(8,128)} %bitcast.14, f32[64,256]{1,0:T(8,128)} %bitcast.19, s32[1,1]{1,0:T(1,128)S(6)} %copy.14.count_in, ...), custom_call_target="tpu_custom_call" | custom-call | tf_op jit(solution)/shard_map/window/pallas_call | solution.py:1448
  19.0 0.8 %keep.1 = (f32[512,256]{1,0:T(8,128)}, f32[8,48]{1,0:T(8,128)}) custom-call(f32[512,256]{1,0:T(8,128)S(1)} %get-tuple-element.6.field_in, f32[8,48]{1,0:T(8,128)S(1)} %get-tuple-element.7.flow_in), custom_call_target="tpu_custom_call" | custom-call | tf_op jit(solution)/shard_map/keep/pallas_call | solution.py:1451

commit v3 on v2

--- a/solution.py
+++ b/solution.py
@@ -1012,7 +1012,7 @@
 
     def chunk_loop(body):
         chunks = width_x // ROWS
-        together = math.gcd(chunks, 4)
+        together = math.gcd(chunks, 8)
 
         def step(c, carry):
             for k in range(together):

time: 20 us -> 19.8 us (0.990)
  no operation moved by 1% of the time
where the time goes in v3:
time: 19.8 us; the launch traced here: 19.7 us
  Pallas kernels  18.4 us (93%)
  between operations  1.29 us (7%)
    pallas_call x1, Pallas kernels, fused_shards(): call(*[x if x.size == 1 else pltpu.with_memory_space_constraint(x, pltpu....  17.6 us
    pallas_call x1, Pallas kernels, fused_shards(): pl.pallas_call(keep, out_shape=(jax.ShapeDtypeStruct(field.shape, F32), j...  0.81 us

profile of v3, /device:TPU:0, one launch (start us, length us, event | category | flops | bytes accessed | tf_op | source)
XLA Modules:
  0.0 19.7 jit_solution(10466322338109026633)
XLA Ops:
  1.3 17.6 %window.1 = (f32[512,256]{1,0:T(8,128)S(1)}, f32[8,48]{1,0:T(8,128)S(1)}) custom-call(f32[512,256]{1,0:T(8,128)} %bitcast.15, f32[512,256]{1,0:T(8,128)} %bitcast.16, f32[512,256]{1,0:T(8,128)} %bitcast.17, f32[512,256]{1,0:T(8,128)} %bitcast.18, f32[4096,256]{1,0:T(8,128)} %bitcast.14, f32[64,256]{1,0:T(8,128)} %bitcast.19, s32[1,1]{1,0:T(1,128)S(6)} %copy.14.count_in, ...), custom_call_target="tpu_custom_call" | custom-call | tf_op jit(solution)/shard_map/window/pallas_call | solution.py:1448
  18.9 0.8 %keep.1 = (f32[512,256]{1,0:T(8,128)}, f32[8,48]{1,0:T(8,128)}) custom-call(f32[512,256]{1,0:T(8,128)S(1)} %get-tuple-element.6.field_in, f32[8,48]{1,0:T(8,128)S(1)} %get-tuple-element.7.flow_in), custom_call_target="tpu_custom_call" | custom-call | tf_op jit(solution)/shard_map/keep/pallas_call | solution.py:1451
